TPU v7x, 32 devices: a whole 2x2x4 slice. The times are simulated.
32 devices in a mesh: head: 8 (over y, x, core), req: 4 (over z).
Axes of the slice: x: 2, y: 2, z: 4, core: 2. Of those that a mesh axis runs over, the one named last changes fastest.
Arguments:
- hidden: bfloat16 [128, 5, 2048], P('req', None, 'head'), may hold values from -6 to 6
- w_key: bfloat16 [2048, 4096], P('head'), may hold values from -0.125 to 0.125
- w_value: bfloat16 [2048, 32, 256], P(None, 'head'), may hold values from -0.125 to 0.125
- w_gates: bfloat16 [2048, 32, 2], P(None, 'head'), may hold values from -0.125 to 0.125
- conv_key: bfloat16 [4, 4096], replicated, may hold values from -3 to 3
- conv_value: bfloat16 [4, 4096], P(None, 'head'), may hold values from -3 to 3
- key_conv_state: bfloat16 [128, 3, 4096], P('req'), may hold values from -6 to 6
- value_conv_state: bfloat16 [128, 3, 4096], P('req', None, 'head'), may hold values from -6 to 6
- states: float32 [128, 32, 128, 128], P('req', 'head'), may hold values from -3 to 3
- a_log: float32 [32], P('head'), may hold values from -1.5 to 1
- dt_bias: float32 [32], P('head'), may hold values from -1 to 1
- norm_weight: float32 [128], replicated, may hold values from 0.1 to 1.9
- w_out: bfloat16 [4096, 2048], P('head'), may hold values from -0.125 to 0.125
- accepted: int32 [128], P('req'), may hold values from 0 to 4
- next_group: int32 [128], P('req'), may hold values from 0 to 3, as said below
- next_slot: int32 [128], P('req'), may hold values from 0 to 31, as said below
Outputs:
- mixed: bfloat16 [128, 5, 2048], P('req', None, 'head')
- new_states: float32 [128, 32, 128, 128], P('req', 'head')
- new_key_conv: bfloat16 [128, 3, 4096], P('req', None, 'head')
- new_value_conv: bfloat16 [128, 3, 4096], P('req', None, 'head')
Inputs may be any that keep to these rules, and one draw needn't show every extreme that they name: `next_group`: within each group's 32 requests at most 12 have the same next group, and in every draw some group sends exactly 12 to one group; every group is named by exactly 32 requests in all. The pairs (next_group, next_slot) are all different.
All inputs are finite; a program needn't handle non-finite values.
Results may differ from a plain program's by a relative error of at most 0.012.
Values may be sent and summed in bfloat16 or wider, within the bound.
A program may use at most 128 MiB of HBM per device.

v0:
```python
import jax
import jax.numpy as jnp
from jax import lax
from jax.sharding import PartitionSpec as P

CAP = 12


def causal_conv(state, raw, taps, window):
    joined = jnp.concatenate([state, raw], axis=1)
    wide = joined.astype(jnp.float32)
    kernel = taps.astype(jnp.float32)
    total = kernel[0][None, None, :] * wide[:, 0:window]
    for index in range(1, taps.shape[0]):
        total = total + kernel[index][None, None, :] * wide[:, index : index + window]
    return (jax.nn.silu(total).astype(jnp.bfloat16), joined)


def keep_tail(joined, accepted, span):
    offsets = accepted[:, None] + 1 + jnp.arange(span, dtype=jnp.int32)[None, :]
    return jnp.take_along_axis(joined, offsets[:, :, None], axis=1)


def unit_norm(vector):
    return vector * lax.rsqrt(jnp.sum(vector * vector, axis=-1, keepdims=True) + 1e-06)


def spread_heads(block, devices, key_heads, pair_width):
    rows = block.shape[0]
    shaped = block.reshape(rows, -1, pair_width)
    wanted = devices * key_heads
    if shaped.shape[1] < wanted:
        shaped = jnp.repeat(shaped, wanted // shaped.shape[1], axis=1)
    return shaped.reshape(rows, wanted * pair_width)


def local(
    hidden,
    w_key,
    w_value,
    w_gates,
    conv_key,
    conv_value,
    key_conv_state,
    value_conv_state,
    states,
    a_log,
    dt_bias,
    norm_weight,
    w_out,
    accepted,
    next_group,
    next_slot,
):
    requests, window, feature_piece = hidden.shape
    total_rows = requests * window
    heads = states.shape[1]
    key_size = states.shape[2]
    value_size = states.shape[3]
    span = key_conv_state.shape[1]
    devices = lax.axis_size("head")
    position = lax.axis_index("head")
    pair_width = 2 * key_size
    key_heads = max(1, heads // 2)
    needed = key_heads * pair_width
    own_width = key_conv_state.shape[2] // devices
    first_head = position * heads // 2
    gathered = lax.all_gather(hidden, "head", axis=2, tiled=True)
    flat = gathered.reshape(total_rows, -1)
    model_width = flat.shape[1]
    spread = spread_heads(w_key, devices, key_heads, pair_width)
    columns = lax.all_to_all(spread, "head", split_axis=1, concat_axis=0, tiled=True)
    keys_raw = jnp.dot(flat, columns, preferred_element_type=jnp.float32).astype(jnp.bfloat16)
    value_raw = jnp.dot(
        flat,
        w_value.reshape(model_width, heads * 2 * value_size),
        preferred_element_type=jnp.float32,
    ).astype(jnp.bfloat16)
    value_raw = value_raw.reshape(requests, window, heads, 2, value_size)
    gate_raw = jnp.dot(
        flat, w_gates.reshape(model_width, heads * 2), preferred_element_type=jnp.float32
    ).astype(jnp.bfloat16)
    gate_raw = gate_raw.reshape(requests, window, heads, 2).astype(jnp.float32)
    column_start = first_head * pair_width
    local_state = lax.dynamic_slice_in_dim(key_conv_state, column_start, needed, 2)
    local_taps = lax.dynamic_slice_in_dim(conv_key, column_start, needed, 1)
    key_out, key_joined = causal_conv(
        local_state, keys_raw.reshape(requests, window, needed), local_taps, window
    )
    v_raw = value_raw[:, :, :, 0].reshape(requests, window, heads * value_size)
    value_out, value_joined = causal_conv(value_conv_state, v_raw, conv_value, window)
    split = key_out.reshape(requests, window, key_heads, 2, key_size).astype(jnp.float32)
    queries = jnp.repeat(
        unit_norm(split[:, :, :, 0]) * key_size ** (-0.5), heads // key_heads, axis=2
    )
    key_rows = jnp.repeat(unit_norm(split[:, :, :, 1]), heads // key_heads, axis=2)
    values = value_out.reshape(requests, window, heads, value_size).astype(jnp.float32)
    beta = jax.nn.sigmoid(gate_raw[..., 0])
    decay = jnp.exp(-jnp.exp(a_log) * jax.nn.softplus(gate_raw[..., 1] + dt_bias))
    current = states
    kept = states
    outputs = []
    for step in range(window):
        current = current * decay[:, step][:, :, None, None]
        guess = jnp.einsum(
            "rhk,rhkv->rhv", key_rows[:, step], current, precision=lax.Precision.HIGHEST
        )
        change = beta[:, step][:, :, None] * (values[:, step] - guess)
        current = current + key_rows[:, step][:, :, :, None] * change[:, :, None, :]
        outputs.append(
            jnp.einsum("rhk,rhkv->rhv", queries[:, step], current, precision=lax.Precision.HIGHEST)
        )
        kept = jnp.where((accepted == step)[:, None, None, None], current, kept)
    core = jnp.stack(outputs, axis=1)
    zgate = value_raw[:, :, :, 1].astype(jnp.float32)
    scaled = core * lax.rsqrt(jnp.mean(core * core, axis=-1, keepdims=True) + 1e-06)
    normed = (scaled * norm_weight * jax.nn.silu(zgate)).astype(jnp.bfloat16)
    partial_out = jnp.dot(
        normed.reshape(total_rows, heads * value_size), w_out, preferred_element_type=jnp.float32
    )
    mixed = lax.psum_scatter(partial_out, "head", scatter_dimension=1, tiled=True).astype(
        jnp.bfloat16
    )
    mixed = mixed.reshape(requests, window, -1)
    key_whole_tail = keep_tail(key_joined, accepted, span)
    own_start = position * own_width - column_start
    key_tail = lax.dynamic_slice_in_dim(key_whole_tail, own_start, own_width, 2)
    value_tail = keep_tail(value_joined, accepted, span)
    groups = lax.axis_size("req")
    capacity = CAP
    onehot = (next_group[:, None] == jnp.arange(groups, dtype=jnp.int32)[None, :]).astype(jnp.int32)
    before = jnp.cumsum(onehot, axis=0) - onehot
    rank = jnp.sum(before * onehot, axis=1)
    matched = (next_group[None, None, :] == jnp.arange(groups, dtype=jnp.int32)[:, None, None]) & (
        rank[None, None, :] == jnp.arange(capacity, dtype=jnp.int32)[None, :, None]
    )
    matched = matched.astype(jnp.int32)
    picked = jnp.sum(
        matched * jnp.arange(requests, dtype=jnp.int32)[None, None, :], axis=2
    ).reshape(-1)
    filled = jnp.sum(matched, axis=2) > 0
    labels = jnp.where(filled, jnp.sum(matched * next_slot[None, None, :], axis=2), requests)
    send_state = jnp.take(kept, picked, axis=0).reshape(
        groups, capacity, heads, key_size, value_size
    )
    send_key = jnp.take(key_tail, picked, axis=0).reshape(groups, capacity, span, own_width)
    send_value = jnp.take(value_tail, picked, axis=0).reshape(
        groups, capacity, span, heads * value_size
    )
    arrived = (
        lax.all_to_all(send_state, "req", split_axis=0, concat_axis=0, tiled=True),
        lax.all_to_all(
            send_key.astype(jnp.float32), "req", split_axis=0, concat_axis=0, tiled=True
        ).astype(send_key.dtype),
        lax.all_to_all(
            send_value.astype(jnp.float32), "req", split_axis=0, concat_axis=0, tiled=True
        ).astype(send_value.dtype),
        lax.all_to_all(labels, "req", split_axis=0, concat_axis=0, tiled=True),
    )
    arrived_labels = arrived[3].reshape(-1)
    incoming = arrived_labels.shape[0]
    owner = jnp.sum(
        jnp.where(
            arrived_labels[None, :] == jnp.arange(requests, dtype=jnp.int32)[:, None],
            jnp.arange(incoming, dtype=jnp.int32)[None, :],
            0,
        ),
        axis=1,
    )
    new_states = jnp.take(arrived[0].reshape(incoming, heads, key_size, value_size), owner, axis=0)
    new_key_conv = jnp.take(arrived[1].reshape(incoming, span, own_width), owner, axis=0)
    new_value_conv = jnp.take(arrived[2].reshape(incoming, span, heads * value_size), owner, axis=0)
    return (mixed, new_states, new_key_conv, new_value_conv)


def solution(mesh):
    in_specs = (
        P("req", None, "head"),
        P("head", None),
        P(None, "head", None),
        P(None, "head", None),
        P(),
        P(None, "head"),
        P("req", None, None),
        P("req", None, "head"),
        P("req", "head", None, None),
        P("head"),
        P("head"),
        P(),
        P("head", None),
        P("req"),
        P("req"),
        P("req"),
    )
    out_specs = (
        P("req", None, "head"),
        P("req", "head", None, None),
        P("req", None, "head"),
        P("req", None, "head"),
    )
    return jax.shard_map(local, mesh=mesh, in_specs=in_specs, out_specs=out_specs, check_vma=False)
```

profile of v0, /device:TPU:0, one launch (start us, length us, event | category | flops | bytes accessed | tf_op | source)
XLA Modules:
  0.0 555.9 jit_solution(13027797005811086945)
XLA Ops:
  7.2 4.2 copy.184
  11.5 5.2 all-to-all-start
  21.4 29.4 %all_gather.3 = bf16[32,5,2048]{2,0,1:T(8,128)(2,1)S(1)} all-gather(bf16[32,5,256]{2,0,1:T(8,128)(2,1)S(1)} %copy-done.26), channel_id=1, replica_groups=mesh['head'=8,'req'=4] {'head'}, dimensions={2}, use_global_device_ids=true | all-gather | bytes 737280 | tf_op jit(solution)/shard_map/all_gather | solution.py:68
  53.7 3.2 copy.248
  75.2 1.7 copy.244
  76.9 1.7 copy.242
  78.7 1.7 copy.240
  80.4 1.7 copy.238
  94.2 2.3 gather_fusion.5
  107.6 5.6 %all-to-all-start.1 = ((s32[4,1,12]{2,1,0:T(1,128)}), s32[4,1,12]{2,1,0:T(1,128)}, u32[]{:S(2)}, u32[]{:S(2)}) async-start(s32[4,1,12]{2,1,0:T(1,128)} %copy.202), calls=%async_computation.2 | async-start | bytes 4096 | tf_op jit(solution)/shard_map/all_to_all | solution.py:158
  113.2 3.9 copy.185
  117.1 2.1 convolution_convert_fusion.1
  127.8 10.3 %fusion.11 = f32[32,4,1,128]{3,2,1,0:T(1,128)S(1)} fusion(f32[32,4,128,1]{2,3,1,0:T(1,128)} %bitcast.248, f32[32,4,128,128]{3,2,1,0:T(8,128)} %param.30, f32[32,4]{1,0:T(8,128)} %bitcast.234), kind=kOutput, calls=%fused_computation.25 | convolution fusion | flops 27262976 | bytes 8520192 | tf_op jit(solution)/shard_map/rhk,rhkv->rhv/dot_general | solution.py:105
  139.0 10.6 %fusion.8 = f32[32,4,1,128]{3,2,1,0:T(1,128)S(1)} fusion(f32[32,4,128,1]{2,3,1,0:T(1,128)S(1)} %bitcast.293, f32[32,4,128,128]{3,2,1,0:T(8,128)} %param.30, f32[32,4]{1,0:T(8,128)} %bitcast.264, f32[32,4,128]{2,1,0:T(4,128)S(1)} %fusion.79, f32[32,4,128]{2,1,0:T(4,128)S(1)} %get-tuple-element.39, f32[32,4]{1,0:T(8,128)} %bitcast.235), kind=kOutput, calls=%fused_computation.22 | convolution fusion | flops 33554432 | bytes 8651776 | tf_op jit(solution)/shard_map/rhk,rhkv->rhv/dot_general | solution.py:105
  149.9 11.9 %fusion.6 = f32[32,4,1,128]{3,2,1,0:T(1,128)S(1)} fusion(f32[32,4,128,1]{2,3,1,0:T(1,128)S(1)} %bitcast.292, f32[32,4,128,128]{3,2,1,0:T(8,128)S(1)} %bitcast.215, f32[32,4]{1,0:T(8,128)S(1)} %bitcast.257, f32[32,4,128]{2,1,0:T(4,128)S(1)} %fusion.77, f32[32,4,128]{2,1,0:T(4,128)S(1)} %get-tuple-element.40, f32[32,4]{1,0:T(8,128)S(1)} %bitcast.265, ...), kind=kOutput, calls=%fused_computation.20 | convolution fusion | flops 39845888 | bytes 8783360 | tf_op jit(solution)/shard_map/rhk,rhkv->rhv/dot_general | solution.py:105
  162.0 16.3 %fusion.3 = f32[32,4,1,128]{3,2,1,0:T(1,128)S(1)} fusion(f32[32,4,128,1]{2,3,1,0:T(1,128)S(1)} %bitcast.291, f32[32,4]{1,0:T(8,128)S(1)} %bitcast.252, f32[32,4,128,128]{3,2,1,0:T(8,128)S(1)} %bitcast.215, f32[32,4,128]{2,1,0:T(4,128)S(1)} %fusion.75, f32[32,4,128]{2,1,0:T(4,128)S(1)} %copy-done.19, f32[32,4]{1,0:T(8,128)S(1)} %bitcast.258, ...), kind=kOutput, calls=%fused_computation.17 | convolution fusion | flops 46137344 | bytes 8914944 | tf_op jit(solution)/shard_map/rhk,rhkv->rhv/dot_general | solution.py:105
  179.5 20.9 %fusion = f32[32,4,1,128]{3,2,1,0:T(1,128)S(1)} fusion(f32[32,4,128,1]{2,3,1,0:T(1,128)S(1)} %bitcast.290, f32[32,4]{1,0:T(8,128)S(1)} %bitcast.249, f32[32,4,128]{2,1,0:T(4,128)S(1)} %fusion.73, f32[32,4,128]{2,1,0:T(4,128)S(1)} %copy-done.22, f32[32,4]{1,0:T(8,128)S(1)} %bitcast.253, f32[32,4,128,128]{3,2,1,0:T(8,128)S(1)} %bitcast.215, ...), kind=kOutput, calls=%fused_computation.14 | convolution fusion | flops 52428800 | bytes 9046528 | tf_op jit(solution)/shard_map/rhk,rhkv->rhv/dot_general | solution.py:105
  200.6 5.1 all-to-all-start.3
  205.7 17.9 %select_select_fusion = f32[32,4,128,128]{3,2,1,0:T(8,128)} fusion(f32[32,4,128,128]{3,2,1,0:T(8,128)} %param.30, f32[32,4,128]{2,1,0:T(4,128)S(1)} %fusion.71, f32[32,4,128]{2,1,0:T(4,128)S(1)} %copy-done.13, f32[32,4]{1,0:T(8,128)S(1)} %bitcast.250, f32[32,4,128]{2,1,0:T(4,128)} %copy-done.9, f32[32,4,128]{2,1,0:T(4,128)S(1)} %copy-done.23, ...), kind=kLoop, calls=%fused_computation.8 | loop fusion | flops 41943040 | bytes 17435296 | tf_op jit(solution)/shard_map/jit(_where)/select_n | solution.py:113
  223.7 11.1 %gather_fusion = f32[48,4,128,128]{3,2,1,0:T(8,128)} fusion(f32[32,4,128,128]{3,2,1,0:T(8,128)} %select_select_fusion, s32[1024]{0:T(1024)} %get-tuple-element.87), kind=kCustom, calls=%fused_computation.6 | custom fusion | bytes 25166016 | tf_op jit(solution)/shard_map/jit(_take)/gather | solution.py:143
  234.8 5.1 all-to-all-start.4
  240.0 12.1 %broadcast_select_fusion = f32[4,12,4,128,128]{4,3,2,1,0:T(8,128)} fusion(f32[4,12,4,128,128]{4,3,2,1,0:T(8,128)} %bitcast.218, pred[4,12]{1,0:T(4,128)(4,1)S(1)} %copy-done.45), kind=kLoop, calls=%fused_computation.27 | loop fusion | flops 3145728 | bytes 25165872 | tf_op jit(solution)/shard_map/jit(_take)/select_n | solution.py:143
  252.1 6.4 %all-to-all-start.2 = ((f32[4,12,4,128,128]{4,3,2,1,0:T(8,128)}), f32[4,12,4,128,128]{4,3,2,1,0:T(8,128)}, u32[]{:S(2)}, u32[]{:S(2)}) async-start(f32[4,12,4,128,128]{4,3,2,1,0:T(8,128)} %broadcast_select_fusion), calls=%async_computation.3 | async-start | bytes 25165824 | tf_op jit(solution)/shard_map/all_to_all | solution.py:151
  260.4 10.5 %fusion.13 = f32[32,4,1,128]{3,2,1,0:T(1,128)S(1)} fusion(f32[32,4,128,1]{2,3,1,0:T(1,128)S(1)} %bitcast.245, f32[32,4,128,128]{3,2,1,0:T(8,128)} %param.30, f32[32,4,128]{2,1,0:T(4,128)S(1)} %fusion.79, f32[32,4,128]{2,1,0:T(4,128)S(1)} %get-tuple-element.39, f32[32,4]{1,0:T(8,128)S(1)} %bitcast.240), kind=kOutput, calls=%fused_computation.28 | convolution fusion | flops 31457280 | bytes 8651264 | tf_op jit(solution)/shard_map/rhk,rhkv->rhv/dot_general | solution.py:111
  271.0 12.5 %fusion.10 = f32[32,4,1,128]{3,2,1,0:T(1,128)S(1)} fusion(f32[32,4,128,1]{2,3,1,0:T(1,128)S(1)} %bitcast.276, f32[32,4,128,128]{3,2,1,0:T(8,128)} %param.30, f32[32,4,128]{2,1,0:T(4,128)S(1)} %copy-done.6, f32[32,4,128]{2,1,0:T(4,128)S(1)} %copy-done.18, f32[32,4]{1,0:T(8,128)S(1)} %bitcast.269, f32[32,4,128]{2,1,0:T(4,128)S(1)} %fusion.79, ...), kind=kOutput, calls=%fused_computation.24 | convolution fusion | flops 37748736 | bytes 8782848 | tf_op jit(solution)/shard_map/rhk,rhkv->rhv/dot_general | solution.py:111
  283.6 15.4 %fusion.97 = f32[32,4,1,128]{3,2,1,0:T(1,128)S(1)} fusion(f32[32,4,128,1]{2,3,1,0:T(1,128)S(1)} %bitcast.275, f32[32,4,128,128]{3,2,1,0:T(8,128)S(1)} %bitcast.217, f32[32,4,128]{2,1,0:T(4,128)S(1)} %copy-done.8, f32[32,4,128]{2,1,0:T(4,128)S(1)} %copy-done.21, f32[32,4]{1,0:T(8,128)S(1)} %bitcast.261, f32[32,4,128]{2,1,0:T(4,128)S(1)} %copy-done.6, ...), kind=kOutput, calls=%fused_computation.199 | convolution fusion | flops 44040192 | bytes 8914432 | tf_op jit(solution)/shard_map/rhk,rhkv->rhv/dot_general | solution.py:111
  299.1 20.7 %fusion.5 = f32[32,4,1,128]{3,2,1,0:T(1,128)S(1)} fusion(f32[32,4,128,1]{2,3,1,0:T(1,128)S(1)} %bitcast.274, f32[32,4,128]{2,1,0:T(4,128)S(1)} %copy-done.10, f32[32,4,128]{2,1,0:T(4,128)S(1)} %copy-done.24, f32[32,4]{1,0:T(8,128)S(1)} %bitcast.255, f32[32,4,128,128]{3,2,1,0:T(8,128)S(1)} %bitcast.217, f32[32,4,128]{2,1,0:T(4,128)S(1)} %copy-done.8, ...), kind=kOutput, calls=%fused_computation.19 | convolution fusion | flops 50331648 | bytes 9046016 | tf_op jit(solution)/shard_map/rhk,rhkv->rhv/dot_general | solution.py:111
  319.9 23.1 %fusion.2 = f32[32,4,1,128]{3,2,1,0:T(1,128)S(1)} fusion(f32[32,4,128,1]{2,3,1,0:T(1,128)S(1)} %bitcast.273, f32[32,4,128]{2,1,0:T(4,128)S(1)} %copy-done.12, f32[32,4,128]{2,1,0:T(4,128)S(1)} %copy-done.14, f32[32,4]{1,0:T(8,128)S(1)} %bitcast.251, f32[32,4,128]{2,1,0:T(4,128)S(1)} %copy-done.10, f32[32,4,128]{2,1,0:T(4,128)S(1)} %copy-done.24, ...), kind=kOutput, calls=%fused_computation.16 | convolution fusion | flops 56623104 | bytes 9177600 | tf_op jit(solution)/shard_map/rhk,rhkv->rhv/dot_general | solution.py:111
  350.2 32.0 %reduce-scatter.2.cloned.1.call-done = f32[160,256]{1,0:T(8,128)} async-done(((f32[160,2048]{1,0:T(8,128)}), f32[160,256]{1,0:T(8,128)}) %reduce-scatter.2.cloned.1.call-update) | async-done | bytes 163856 | tf_op jit(solution)/shard_map/reduce_scatter | solution.py:121
  383.8 147.2 %all-to-all-done.2 = f32[4,12,4,128,128]{4,3,2,1,0:T(8,128)} async-done(((f32[4,12,4,128,128]{4,3,2,1,0:T(8,128)}), f32[4,12,4,128,128]{4,3,2,1,0:T(8,128)}, u32[]{:S(2)}, u32[]{:S(2)}) %all-to-all-start.2) | async-done | bytes 12582944 | tf_op jit(solution)/shard_map/all_to_all | solution.py:151
  531.0 9.1 %gather_fusion.1 = f32[32,4,128,128]{3,2,1,0:T(8,128)} fusion(f32[48,4,128,128]{3,2,1,0:T(8,128)} %bitcast.91, s32[1024]{0:T(1024)S(1)} %pad_clamp_fusion.2), kind=kCustom, calls=%fused_computation.7 | custom fusion | bytes 16777344 | tf_op jit(solution)/shard_map/jit(_take)/gather | solution.py:170
  540.0 8.6 %broadcast_select_fusion.1 = f32[32,4,128,128]{3,2,1,0:T(8,128)} fusion(f32[32,4,128,128]{3,2,1,0:T(8,128)} %gather_fusion.1, pred[32]{0:T(512)(128)(4,1)S(1)} %compare_and_fusion.2), kind=kLoop, calls=%fused_computation.29 | loop fusion | flops 2097152 | bytes 16777248 | tf_op jit(solution)/shard_map/jit(_take)/select_n | solution.py:170
  (232 shorter events, 70.4 us)
Async XLA Ops:
  7.2 336.4 %copy-start = (bf16[512,2048]{1,0:T(8,128)(2,1)S(1)}, bf16[512,2048]{1,0:T(8,128)(2,1)}, u32[]{:S(2)}) copy-start(bf16[512,2048]{1,0:T(8,128)(2,1)} %param.34) | copy-start | bytes 6291460
  11.5 96.1 %all-to-all-start = ((bf16[256,8,512]{0,2,1:T(8,128)(2,1)}), bf16[256,8,512]{0,2,1:T(8,128)(2,1)}, u32[]{:S(2)}, u32[]{:S(2)}) async-start(bf16[256,8,512]{0,2,1:T(8,128)(2,1)} %bitcast.220), calls=%async_computation | async-start | bytes 4194304 | tf_op jit(solution)/shard_map/all_to_all | solution.py:72
  107.6 93.0 %all-to-all-start.1 = ((s32[4,1,12]{2,1,0:T(1,128)}), s32[4,1,12]{2,1,0:T(1,128)}, u32[]{:S(2)}, u32[]{:S(2)}) async-start(s32[4,1,12]{2,1,0:T(1,128)} %copy.202), calls=%async_computation.2 | async-start | bytes 4096 | tf_op jit(solution)/shard_map/all_to_all | solution.py:158
  124.7 25.0 %copy-start.15 = (f32[32,4,128]{2,1,0:T(4,128)}, f32[32,4,128]{2,1,0:T(4,128)S(1)}, u32[]{:S(2)}) copy-start(f32[32,4,128]{2,1,0:T(4,128)S(1)} %get-tuple-element.40) | copy-start | bytes 196612
  127.8 21.9 %copy-start.35 = (f32[32,1,4]{2,0,1:T(8,128)S(1)}, f32[32,1,4]{2,0,1:T(8,128)}, u32[]{:S(2)}) copy-start(f32[32,1,4]{2,0,1:T(8,128)} %copy.238) | copy-start | bytes 1540
  127.8 22.0 %slice-start = ((s8[8388608]{0:T(1024)(128)(4,1)}), s8[4194304]{0:T(1024)(128)(4,1)S(1)}, s32[]{:S(2)}) async-start(s8[8388608]{0:T(1024)(128)(4,1)} %bitcast.214), calls=%async_computation.7 | async-start | bytes 8388608
  127.8 22.0 %copy-start.4 = (f32[32,1,4]{2,0,1:T(8,128)S(1)}, f32[32,1,4]{2,0,1:T(8,128)}, u32[]{:S(2)}) copy-start(f32[32,1,4]{2,0,1:T(8,128)} %copy.235) | copy-start | bytes 1540
  127.8 22.0 %copy-start.29 = (f32[32,1,4]{2,0,1:T(8,128)S(1)}, f32[32,1,4]{2,0,1:T(8,128)}, u32[]{:S(2)}) copy-start(f32[32,1,4]{2,0,1:T(8,128)} %copy.239) | copy-start | bytes 1540
  127.8 22.0 %copy-start.30 = (f32[32,1,4]{2,0,1:T(8,128)S(1)}, f32[32,1,4]{2,0,1:T(8,128)}, u32[]{:S(2)}) copy-start(f32[32,1,4]{2,0,1:T(8,128)} %copy.237) | copy-start | bytes 1540
  127.8 22.0 %copy-start.38 = (f32[32,1,4,128]{3,2,0,1:T(4,128)S(1)}, f32[32,1,4,128]{3,2,0,1:T(4,128)}, u32[]{:S(2)}) copy-start(f32[32,1,4,128]{3,2,0,1:T(4,128)} %get-tuple-element.45) | copy-start | bytes 196612
  149.7 55.9 %copy-start.5 = (f32[32,4,128]{2,1,0:T(4,128)}, f32[32,4,128]{2,1,0:T(4,128)S(1)}, u32[]{:S(2)}) copy-start(f32[32,4,128]{2,1,0:T(4,128)S(1)} %fusion.77) | copy-start | bytes 196612
  161.9 43.8 %copy-start.7 = (f32[32,4,128]{2,1,0:T(4,128)}, f32[32,4,128]{2,1,0:T(4,128)S(1)}, u32[]{:S(2)}) copy-start(f32[32,4,128]{2,1,0:T(4,128)S(1)} %fusion.75) | copy-start | bytes 196612
  161.9 17.5 %copy-start.16 = (f32[32,4,128]{2,1,0:T(4,128)S(1)}, f32[32,4,128]{2,1,0:T(4,128)}, u32[]{:S(2)}) copy-start(f32[32,4,128]{2,1,0:T(4,128)} %copy-done.15) | copy-start | bytes 196612
  161.9 17.5 %copy-start.22 = (f32[32,4,128]{2,1,0:T(4,128)S(1)}, f32[32,4,128]{2,1,0:T(4,128)}, u32[]{:S(2)}) copy-start(f32[32,4,128]{2,1,0:T(4,128)} %get-tuple-element.42) | copy-start | bytes 196612
  161.9 17.5 %copy-start.27 = (f32[32,1,4]{2,0,1:T(8,128)S(1)}, f32[32,1,4]{2,0,1:T(8,128)}, u32[]{:S(2)}) copy-start(f32[32,1,4]{2,0,1:T(8,128)} %copy.243) | copy-start | bytes 1540
  178.4 22.1 %copy-start.9 = (f32[32,4,128]{2,1,0:T(4,128)}, f32[32,4,128]{2,1,0:T(4,128)S(1)}, u32[]{:S(2)}) copy-start(f32[32,4,128]{2,1,0:T(4,128)S(1)} %fusion.73) | copy-start | bytes 196612
  179.4 21.0 %copy-start.32 = (f32[32,1,4]{2,0,1:T(8,128)S(1)}, f32[32,1,4]{2,0,1:T(8,128)}, u32[]{:S(2)}) copy-start(f32[32,1,4]{2,0,1:T(8,128)} %copy.244) | copy-start | bytes 1540
  179.4 26.2 %copy-start.13 = (f32[32,4,128]{2,1,0:T(4,128)S(1)}, f32[32,4,128]{2,1,0:T(4,128)}, u32[]{:S(2)}) copy-start(f32[32,4,128]{2,1,0:T(4,128)} %get-tuple-element.38) | copy-start | bytes 196612
  179.4 26.2 %copy-start.17 = (f32[32,4,128]{2,1,0:T(4,128)S(1)}, f32[32,4,128]{2,1,0:T(4,128)}, u32[]{:S(2)}) copy-start(f32[32,4,128]{2,1,0:T(4,128)} %copy-done.15) | copy-start | bytes 196612
  179.5 26.2 %copy-start.20 = (f32[32,4,128]{2,1,0:T(4,128)S(1)}, f32[32,4,128]{2,1,0:T(4,128)}, u32[]{:S(2)}) copy-start(f32[32,4,128]{2,1,0:T(4,128)} %get-tuple-element.41) | copy-start | bytes 196612
  179.5 26.2 %copy-start.23 = (f32[32,4,128]{2,1,0:T(4,128)S(1)}, f32[32,4,128]{2,1,0:T(4,128)}, u32[]{:S(2)}) copy-start(f32[32,4,128]{2,1,0:T(4,128)} %get-tuple-element.42) | copy-start | bytes 196612
  179.5 26.2 %copy-start.41 = (pred[32]{0:T(512)(128)(4,1)S(1)}, pred[32]{0:T(512)(128)(4,1)}, u32[]{:S(2)}) copy-start(pred[32]{0:T(512)(128)(4,1)} %get-tuple-element.81) | copy-start | bytes 100
  179.5 26.2 %copy-start.42 = (pred[32]{0:T(512)(128)(4,1)S(1)}, pred[32]{0:T(512)(128)(4,1)}, u32[]{:S(2)}) copy-start(pred[32]{0:T(512)(128)(4,1)} %get-tuple-element.82) | copy-start | bytes 100
  179.5 26.2 %copy-start.43 = (pred[32]{0:T(512)(128)(4,1)S(1)}, pred[32]{0:T(512)(128)(4,1)}, u32[]{:S(2)}) copy-start(pred[32]{0:T(512)(128)(4,1)} %get-tuple-element.83) | copy-start | bytes 100
  179.5 26.2 %copy-start.44 = (pred[32]{0:T(512)(128)(4,1)S(1)}, pred[32]{0:T(512)(128)(4,1)}, u32[]{:S(2)}) copy-start(pred[32]{0:T(512)(128)(4,1)} %get-tuple-element.84) | copy-start | bytes 100
  200.5 23.1 %copy-start.11 = (f32[32,4,128]{2,1,0:T(4,128)}, f32[32,4,128]{2,1,0:T(4,128)S(1)}, u32[]{:S(2)}) copy-start(f32[32,4,128]{2,1,0:T(4,128)S(1)} %fusion.71) | copy-start | bytes 196612
  200.6 34.3 %all-to-all-start.3 = ((bf16[4,12,3,512]{3,2,1,0:T(4,128)(2,1)}), bf16[4,12,3,512]{3,2,1,0:T(4,128)(2,1)S(1)}, u32[]{:S(2)}, u32[]{:S(2)}) async-start(bf16[4,12,3,512]{3,2,1,0:T(4,128)(2,1)} %bitcast.110), calls=%async_computation.4 | async-start | bytes 393216 | tf_op jit(solution)/shard_map/all_to_all | solution.py:152
  234.8 17.2 %all-to-all-start.4 = ((bf16[4,12,3,512]{3,2,1,0:T(4,128)(2,1)}), bf16[4,12,3,512]{3,2,1,0:T(4,128)(2,1)S(1)}, u32[]{:S(2)}, u32[]{:S(2)}) async-start(bf16[4,12,3,512]{3,2,1,0:T(4,128)(2,1)} %bitcast.111), calls=%async_computation.5 | async-start | bytes 393216 | tf_op jit(solution)/shard_map/all_to_all | solution.py:155
  252.1 278.9 %all-to-all-start.2 = ((f32[4,12,4,128,128]{4,3,2,1,0:T(8,128)}), f32[4,12,4,128,128]{4,3,2,1,0:T(8,128)}, u32[]{:S(2)}, u32[]{:S(2)}) async-start(f32[4,12,4,128,128]{4,3,2,1,0:T(8,128)} %broadcast_select_fusion), calls=%async_computation.3 | async-start | bytes 25165824 | tf_op jit(solution)/shard_map/all_to_all | solution.py:151
  258.5 123.6 %reduce-scatter.2.cloned.1.call-start = ((), (), s32[]{:S(2)}) async-start(), calls=%async_computation.6 | async-start | bytes 1474560 | tf_op jit(solution)/shard_map/reduce_scatter | solution.py:121
  299.1 20.8 %copy-start.12 = (f32[32,4,128]{2,1,0:T(4,128)S(1)}, f32[32,4,128]{2,1,0:T(4,128)}, u32[]{:S(2)}) copy-start(f32[32,4,128]{2,1,0:T(4,128)} %copy-done.11) | copy-start | bytes 196612
  299.1 20.8 %copy-start.14 = (f32[32,4,128]{2,1,0:T(4,128)S(1)}, f32[32,4,128]{2,1,0:T(4,128)}, u32[]{:S(2)}) copy-start(f32[32,4,128]{2,1,0:T(4,128)} %get-tuple-element.38) | copy-start | bytes 196612
  (30 other events, 353.3 us)
Sparse Core Ops, SparseCore 0:
  345.3 36.8 reduce-scatter.1
where the time goes:
time: 565 us; the launch traced here: 556 us
  waiting for transfers between devices  179 us (32%)
  matrix products  159 us (28%)
  local copies, waits for them, and re-layouts  83.4 us (15%)
  other arithmetic  62 us (11%)
  blocking collectives  29.4 us (5%)
  starting transfers between devices  27.5 us (5%)
  between operations  15.8 us (3%)
    all_to_all x1, waiting for transfers between devices, local(): lax.all_to_all(send_state, 'req', split_axis=0, concat_axis=0, tiled=True)  147 us
    dot_general x5, matrix products, local(): jnp.einsum('rhk,rhkv->rhv', queries[:, step], current, precision=lax.Prec...  82.2 us
    dot_general x5, matrix products, local(): jnp.einsum('rhk,rhkv->rhv', key_rows[:, step], current, precision=lax.Pre...  70 us
    reduce_scatter x1, waiting for transfers between devices, local(): lax.psum_scatter(partial_out, 'head', scatter_dimension=1, tiled=True)  32 us
    all_gather x1, blocking collectives, local(): gathered = lax.all_gather(hidden, 'head', axis=2, tiled=True)  29.4 us
    select_n x1, other arithmetic, local(): kept = jnp.where((accepted == step)[:, None, None, None], current, kept)  17.9 us
    select_n x2, other arithmetic, local(): jnp.take(kept, picked, axis=0)  12.8 us
    unnamed x123, local copies, waits for them, and re-layouts  11.3 us
  transfers between devices with their start and end apart: 6, of which 2 were waited for; matrix products, arithmetic and copies ran while one was open for 51% of the time, Pallas kernels for 0%

commit v1 on v0

v1 whole, which is shorter than its diff:
```python
import functools

import jax
import jax.numpy as jnp
from jax import lax
from jax.experimental import pallas as pl
from jax.experimental.pallas import tpu as pltpu
from jax.sharding import PartitionSpec as P

CAP = 12
F32 = jnp.float32
BF16 = jnp.bfloat16


def spread_heads(block, devices, key_heads, pair_width):
    rows = block.shape[0]
    shaped = block.reshape(rows, -1, pair_width)
    wanted = devices * key_heads
    if shaped.shape[1] < wanted:
        shaped = jnp.repeat(shaped, wanted // shaped.shape[1], axis=1)
    return shaped.reshape(rows, wanted * pair_width)


def silu(x):
    return x / (1.0 + jnp.exp(-x))


def pack_kernel(index_ref, in_ref, out_ref):
    out_ref[...] = in_ref[...].astype(out_ref.dtype)


def pack(states, picked):
    count = picked.shape[0]
    block = (1,) + states.shape[1:]
    zeros = (0,) * (states.ndim - 1)
    return pl.pallas_call(
        pack_kernel,
        out_shape=jax.ShapeDtypeStruct((count,) + states.shape[1:], BF16),
        grid_spec=pltpu.PrefetchScalarGridSpec(
            num_scalar_prefetch=1,
            grid=(count,),
            in_specs=[pl.BlockSpec(block, lambda i, index: (index[i],) + zeros)],
            out_specs=pl.BlockSpec(block, lambda i, index: (i,) + zeros),
        ),
        name="pack_states",
    )(picked, states)


def layout(key_heads, heads, window, span, size, needed):
    keys = 0
    deltas = keys + key_heads * window * size
    scale = deltas + heads * window * size
    key_tail = scale + heads * size
    value_tail = key_tail + span * needed
    return keys, deltas, scale, key_tail, value_tail, value_tail + span * heads * size


def verify_kernel(
    dims,
    x_ref,
    wk_ref,
    wv_ref,
    wg_ref,
    ck_ref,
    cv_ref,
    ks_ref,
    vs_ref,
    al_ref,
    db_ref,
    nw_ref,
    acc_ref,
    oh_ref,
    st_ref,
    normed_ref,
    pay_ref,
    kq_s,
    g_s,
    v_s,
    z_s,
    beta_s,
    decay_s,
    p_s,
):
    requests, window, heads, key_heads, size, span, needed, batch, slots = dims
    half = slots // 2
    ratio = heads // key_heads
    devices, _, piece = x_ref.shape
    o_key, o_delta, o_scale, o_kt, o_vt, _ = layout(key_heads, heads, window, span, size, needed)
    step = pl.program_id(0)

    def project(w_ref, lo, width):
        total = jnp.dot(
            x_ref[0], w_ref[0:piece, lo : lo + width], preferred_element_type=F32
        )
        for d in range(1, devices):
            total = total + jnp.dot(
                x_ref[d],
                w_ref[d * piece : (d + 1) * piece, lo : lo + width],
                preferred_element_type=F32,
            )
        return total.astype(BF16).astype(F32)

    def conv(state_ref, taps_ref, raw, lo, width, tail_at, tail_width):
        u = [state_ref[i, :, lo : lo + width].astype(F32) for i in range(span)]
        u += [raw[t * requests : (t + 1) * requests] for t in range(window)]
        outs = []
        for t in range(window):
            total = taps_ref[0:1, lo : lo + width].astype(F32) * u[t]
            for i in range(1, span + 1):
                total = total + taps_ref[i : i + 1, lo : lo + width].astype(F32) * u[t + i]
            outs.append(silu(total).astype(BF16).astype(F32))
        accepted = acc_ref[...]
        for i in range(span):
            tail = u[1 + i]
            for a in range(1, window):
                tail = jnp.where(accepted == a, u[a + 1 + i], tail)
            at = tail_at + i * tail_width + lo
            p_s[:, at : at + width] = tail.astype(BF16)
        return outs

    @pl.when(step == 0)
    def _():
        kq_s[...] = jnp.zeros_like(kq_s)
        for kh in range(key_heads):
            width = 2 * size
            raw = project(wk_ref, kh * width, width)
            outs = conv(ks_ref, ck_ref, raw, kh * width, width, o_kt, needed)
            for t in range(window):
                q = outs[t][:, :size]
                k = outs[t][:, size:]
                q = q * lax.rsqrt(jnp.sum(q * q, axis=-1, keepdims=True) + 1e-06)
                k = k * lax.rsqrt(jnp.sum(k * k, axis=-1, keepdims=True) + 1e-06)
                kq_s[kh, pl.ds(t, requests, stride=slots), :] = k
                kq_s[kh, pl.ds(half + t, requests, stride=slots), :] = q * size ** (-0.5)
        for h in range(heads):
            raw = project(wv_ref, h * 2 * size, 2 * size)
            zg = raw[:, size:]
            z_s[:, h * size : (h + 1) * size] = silu(zg)
            outs = conv(vs_ref, cv_ref, raw[:, :size], h * size, size, o_vt, heads * size)
            for t in range(window):
                v_s[t * requests : (t + 1) * requests, h * size : (h + 1) * size] = outs[t]
        gates = project(wg_ref, 0, 2 * heads)
        beta_s[...] = 1.0 / (1.0 + jnp.exp(-gates))
        shifted = gates + db_ref[...]
        soft = jnp.maximum(shifted, 0.0) + jnp.log1p(jnp.exp(-jnp.abs(shifted)))
        decay_s[...] = jnp.exp(-jnp.exp(al_ref[...]) * soft)

    for rr in range(batch):
        row = pl.multiple_of((step * batch + rr) * slots, slots)
        for kh in range(key_heads):
            lhs = kq_s[kh, pl.ds(row, slots), :].astype(BF16)
            rhs = jnp.concatenate(
                [st_ref[rr, kh * ratio + e].astype(BF16) for e in range(ratio)], axis=1
            )
            got = jnp.dot(lhs, rhs, preferred_element_type=F32)
            for e in range(ratio):
                g_s[kh * ratio + e, pl.ds(row, slots), :] = got[:, e * size : (e + 1) * size]

    @pl.when(step == pl.num_programs(0) - 1)
    def _():
        accepted = acc_ref[...]
        gain = nw_ref[...]
        for kh in range(key_heads):
            ks = [kq_s[kh, pl.ds(t, requests, stride=slots), :] for t in range(window)]
            qs = [kq_s[kh, pl.ds(half + t, requests, stride=slots), :] for t in range(window)]
            kk = {}
            kq = {}
            for t in range(window):
                at = o_key + (kh * window + t) * size
                p_s[:, at : at + size] = ks[t].astype(BF16)
                for j in range(t + 1):
                    if j < t:
                        kk[t, j] = jnp.sum(ks[t] * ks[j], axis=-1, keepdims=True)
                    kq[t, j] = jnp.sum(qs[t] * ks[j], axis=-1, keepdims=True)
            for e in range(ratio):
                h = kh * ratio + e
                cols = slice(h * size, (h + 1) * size)
                deltas = []
                coef = []
                whole = None
                kept_coef = [None] * window
                kept_whole = None
                for t in range(window):
                    rows = slice(t * requests, (t + 1) * requests)
                    beta = beta_s[rows, 2 * h : 2 * h + 1]
                    decay = decay_s[rows, 2 * h + 1 : 2 * h + 2]
                    whole = decay if t == 0 else whole * decay
                    coef = [c * decay for c in coef]
                    guess = whole * g_s[h, pl.ds(t, requests, stride=slots), :]
                    core = whole * g_s[h, pl.ds(half + t, requests, stride=slots), :]
                    for j in range(t):
                        guess = guess + (coef[j] * kk[t, j]) * deltas[j]
                        core = core + (coef[j] * kq[t, j]) * deltas[j]
                    delta = beta * (v_s[rows, cols] - guess)
                    core = core + kq[t, t] * delta
                    deltas.append(delta)
                    coef.append(jnp.ones_like(decay))
                    here = accepted == t
                    kept_whole = whole if t == 0 else jnp.where(here, whole, kept_whole)
                    for j in range(t + 1):
                        before = kept_coef[j] if kept_coef[j] is not None else jnp.zeros_like(decay)
                        kept_coef[j] = jnp.where(here, coef[j], before)
                    scaled = core * lax.rsqrt(
                        jnp.mean(core * core, axis=-1, keepdims=True) + 1e-06
                    )
                    normed_ref[rows, cols] = (scaled * gain * z_s[rows, cols]).astype(BF16)
                for j in range(window):
                    at = o_delta + (h * window + j) * size
                    p_s[:, at : at + size] = (kept_coef[j] * deltas[j]).astype(BF16)
                at = o_scale + h * size
                p_s[:, at : at + size] = jnp.broadcast_to(kept_whole, (requests, size)).astype(BF16)
        pay_ref[...] = jnp.dot(oh_ref[...], p_s[...], preferred_element_type=F32).astype(BF16)


def verify(dims, x, wk, wv, wg, ck, cv, ks, vs, al, db, nw, acc, oh, states):
    requests, window, heads, key_heads, size, span, needed, batch, slots = dims
    rows = requests * window
    width = layout(key_heads, heads, window, span, size, needed)[-1]
    small = [x, wk, wv, wg, ck, cv, ks, vs, al, db, nw, acc, oh]

    def whole(shape):
        return pl.BlockSpec(
            shape, lambda i, n=len(shape): (0,) * n, pipeline_mode=pl.Buffered(1)
        )

    return pl.pallas_call(
        functools.partial(verify_kernel, dims),
        out_shape=(
            jax.ShapeDtypeStruct((rows, heads * size), BF16),
            jax.ShapeDtypeStruct((oh.shape[0], width), BF16),
        ),
        grid=(requests // batch,),
        in_specs=[whole(a.shape) for a in small]
        + [pl.BlockSpec((batch,) + states.shape[1:], lambda i: (i, 0, 0, 0))],
        out_specs=(
            pl.BlockSpec((rows, heads * size), lambda i: (0, 0)),
            pl.BlockSpec((oh.shape[0], width), lambda i: (0, 0)),
        ),
        scratch_shapes=[
            pltpu.VMEM((key_heads, requests * slots, size), F32),
            pltpu.VMEM((heads, requests * slots, size), F32),
            pltpu.VMEM((rows, heads * size), F32),
            pltpu.VMEM((rows, heads * size), F32),
            pltpu.VMEM((rows, 2 * heads), F32),
            pltpu.VMEM((rows, 2 * heads), F32),
            pltpu.VMEM((requests, width), BF16),
        ],
        compiler_params=pltpu.CompilerParams(vmem_limit_bytes=40 * 1024 * 1024),
        name="verify_window",
    )(*small, states)


def place_kernel(
    dims,
    kind_ref,
    own_index,
    base_index,
    extra_index,
    oh_ref,
    pay_ref,
    st_ref,
    base_ref,
    extra_ref,
    out_ref,
    kt_ref,
    vt_ref,
    k_s,
    d_s,
    w_s,
):
    requests, window, heads, key_heads, size, span, needed, lines = dims
    ratio = heads // key_heads
    o_key, o_delta, o_scale, o_kt, o_vt, width = layout(
        key_heads, heads, window, span, size, needed
    )
    step = pl.program_id(0)

    @pl.when(step == 0)
    def _():
        k_s[...] = jnp.zeros_like(k_s)
        d_s[...] = jnp.zeros_like(d_s)

        def columns(lo, hi):
            return jnp.dot(oh_ref[...], pay_ref[:, lo:hi], preferred_element_type=F32)

        for kh in range(key_heads):
            for j in range(window):
                at = o_key + (kh * window + j) * size
                k_s[kh, pl.ds(j, requests, stride=lines), :] = columns(at, at + size)
        for h in range(heads):
            for j in range(window):
                at = o_delta + (h * window + j) * size
                d_s[h, pl.ds(j, requests, stride=lines), :] = columns(at, at + size)
            at = o_scale + h * size
            w_s[h] = columns(at, at + size)
        kt_ref[...] = columns(o_kt, o_vt).astype(BF16)
        vt_ref[...] = columns(o_vt, width).astype(BF16)

    def apply(source_ref):
        row = pl.multiple_of(step * lines, lines)
        for h in range(heads):
            k = k_s[h // ratio, pl.ds(row, lines), :].astype(BF16)
            d = d_s[h, pl.ds(row, lines), :].astype(BF16)
            update = lax.dot_general(
                k, d, (((0,), (0,)), ((), ())), preferred_element_type=F32
            )
            weight = w_s[h, pl.ds(step, 1), :]
            out_ref[0, h] = weight * source_ref[0, h].astype(F32) + update

    kind = kind_ref[step]
    for value, source_ref in enumerate((st_ref, base_ref, extra_ref)):

        @pl.when(kind == value)
        def _(source_ref=source_ref):
            apply(source_ref)


def place(dims, kind, own_i, base_i, extra_i, oh, pay, states, base, extra):
    requests, window, heads, key_heads, size, span, needed, lines = dims
    block = (1,) + states.shape[1:]

    def whole(shape):
        return pl.BlockSpec(
            shape, lambda i, *_, n=len(shape): (0,) * n, pipeline_mode=pl.Buffered(1)
        )

    return pl.pallas_call(
        functools.partial(place_kernel, dims),
        out_shape=(
            jax.ShapeDtypeStruct(states.shape, F32),
            jax.ShapeDtypeStruct((requests, span * needed), BF16),
            jax.ShapeDtypeStruct((requests, span * heads * size), BF16),
        ),
        grid_spec=pltpu.PrefetchScalarGridSpec(
            num_scalar_prefetch=4,
            grid=(requests,),
            in_specs=[
                whole(oh.shape),
                whole(pay.shape),
                pl.BlockSpec(block, lambda i, kind, a, b, c: (a[i], 0, 0, 0)),
                pl.BlockSpec(block, lambda i, kind, a, b, c: (b[i], 0, 0, 0)),
                pl.BlockSpec(block, lambda i, kind, a, b, c: (c[i], 0, 0, 0)),
            ],
            out_specs=(
                pl.BlockSpec(block, lambda i, *_: (i, 0, 0, 0)),
                pl.BlockSpec((requests, span * needed), lambda i, *_: (0, 0)),
                pl.BlockSpec((requests, span * heads * size), lambda i, *_: (0, 0)),
            ),
            scratch_shapes=[
                pltpu.VMEM((key_heads, requests * lines, size), F32),
                pltpu.VMEM((heads, requests * lines, size), F32),
                pltpu.VMEM((heads, requests, size), F32),
            ],
        ),
        compiler_params=pltpu.CompilerParams(vmem_limit_bytes=32 * 1024 * 1024),
        name="place_states",
    )(kind, own_i, base_i, extra_i, oh, pay, states, base, extra)


def local(
    hidden,
    w_key,
    w_value,
    w_gates,
    conv_key,
    conv_value,
    key_conv_state,
    value_conv_state,
    states,
    a_log,
    dt_bias,
    norm_weight,
    w_out,
    accepted,
    next_group,
    next_slot,
):
    requests, window, feature_piece = hidden.shape
    rows = requests * window
    heads = states.shape[1]
    size = states.shape[2]
    span = key_conv_state.shape[1]
    devices = lax.axis_size("head")
    position = lax.axis_index("head")
    groups = lax.axis_size("req")
    group = lax.axis_index("req")
    pair_width = 2 * size
    key_heads = max(1, heads // 2)
    needed = key_heads * pair_width
    own_width = key_conv_state.shape[2] // devices
    column_start = (position * heads // 2) * pair_width
    share = min(CAP, requests // groups)
    extra = CAP - share

    onehot = (next_group[:, None] == jnp.arange(groups, dtype=jnp.int32)[None, :]).astype(jnp.int32)
    before = jnp.cumsum(onehot, axis=0) - onehot
    rank = jnp.sum(before * onehot, axis=1)
    matched = (next_group[None, None, :] == jnp.arange(groups, dtype=jnp.int32)[:, None, None]) & (
        rank[None, None, :] == jnp.arange(CAP, dtype=jnp.int32)[None, :, None]
    )
    picked = jnp.sum(
        matched.astype(jnp.int32) * jnp.arange(requests, dtype=jnp.int32)[None, None, :], axis=2
    )

    base_send = pack(states, picked[:, :share].reshape(-1))
    base = lax.all_to_all(base_send, "req", split_axis=0, concat_axis=0, tiled=True)

    gathered = lax.all_gather(jnp.swapaxes(hidden, 0, 1).reshape(rows, feature_piece), "head", axis=0)
    spread = spread_heads(w_key, devices, key_heads, pair_width)
    columns = lax.all_to_all(spread, "head", split_axis=1, concat_axis=0, tiled=True)
    plan = lax.all_gather(jnp.stack([next_group, next_slot]), "req", axis=0)

    local_state = lax.dynamic_slice_in_dim(key_conv_state, column_start, needed, 2)
    local_taps = lax.dynamic_slice_in_dim(conv_key, column_start, needed, 1)
    send_rows = matched.reshape(groups * CAP, requests).astype(BF16)
    dims = (requests, window, heads, key_heads, size, span, needed, min(8, requests), 16)
    normed, pay = verify(
        dims,
        gathered,
        columns,
        w_value.reshape(devices * feature_piece, heads * 2 * size),
        w_gates.reshape(devices * feature_piece, heads * 2),
        local_taps,
        conv_value,
        jnp.swapaxes(local_state, 0, 1),
        jnp.swapaxes(value_conv_state, 0, 1),
        jnp.repeat(a_log, 2)[None, :],
        jnp.repeat(dt_bias, 2)[None, :],
        norm_weight[None, :],
        accepted[:, None],
        send_rows,
        states,
    )
    partial_out = jnp.dot(normed, w_out, preferred_element_type=F32)
    mixed = lax.psum_scatter(partial_out, "head", scatter_dimension=1, tiled=True).astype(BF16)
    mixed = jnp.swapaxes(mixed.reshape(window, requests, -1), 0, 1)
    pay_in = lax.all_to_all(pay, "req", split_axis=0, concat_axis=0, tiled=True)

    groups_of, slots_of = plan[:, 0], plan[:, 1]
    mine = (groups_of == group).astype(jnp.int32)
    ranks = jnp.cumsum(mine, axis=1) - mine
    hit = (mine[None] > 0) & (slots_of[None] == jnp.arange(requests, dtype=jnp.int32)[:, None, None])
    hit = hit.astype(jnp.int32)
    source = jnp.sum(hit * jnp.arange(groups, dtype=jnp.int32)[None, :, None], axis=(1, 2))
    place_rank = jnp.sum(hit * ranks[None], axis=(1, 2))
    origin = jnp.sum(hit * jnp.arange(requests, dtype=jnp.int32)[None, None, :], axis=(1, 2))
    row_of = source * CAP + place_rank
    take_rows = (row_of[:, None] == jnp.arange(groups * CAP, dtype=jnp.int32)[None, :]).astype(BF16)
    kind = jnp.where(source == group, 0, jnp.where(place_rank < share, 1, 2)).astype(jnp.int32)
    shift_in = (group - source + groups) % groups

    counts = jnp.sum(
        (groups_of[:, None, :] == jnp.arange(groups, dtype=jnp.int32)[None, :, None]).astype(
            jnp.int32
        ),
        axis=2,
    )
    shifts = (
        jnp.arange(groups, dtype=jnp.int32)[None, :]
        - jnp.arange(groups, dtype=jnp.int32)[:, None]
        + groups
    ) % groups
    extra_block = (max(extra, 1),) + states.shape[1:]
    late = []
    pick_extra = picked[:, share:]
    pick_extra, counts, partial_out, pay = lax.optimization_barrier(
        (pick_extra, counts, partial_out, pay)
    )
    for shift in range(1, groups):
        most = jnp.max(jnp.where(shifts == shift, counts, 0))
        pairs = [(s, (s + shift) % groups) for s in range(groups)]

        def send(pick, source_states, pairs=pairs, shift=shift):
            rows_out = lax.dynamic_index_in_dim(pick, (group + shift) % groups, 0, keepdims=False)
            return lax.ppermute(pack(source_states, rows_out), "req", pairs)

        def skip(pick, source_states):
            return jnp.zeros(extra_block, BF16)

        if extra > 0:
            late.append(lax.cond(most > share, send, skip, pick_extra, states))
        else:
            late.append(jnp.zeros(extra_block, BF16))
    late = jnp.concatenate(late, axis=0)

    own_i = jnp.where(kind == 0, origin, 0).astype(jnp.int32)
    base_i = jnp.where(kind == 1, source * share + place_rank, 0).astype(jnp.int32)
    extra_i = jnp.where(
        kind == 2, (shift_in - 1) * extra_block[0] + place_rank - share, 0
    ).astype(jnp.int32)
    dims = (requests, window, heads, key_heads, size, span, needed, 8)
    new_states, key_rows, value_rows = place(
        dims, kind, own_i, base_i, extra_i, take_rows, pay_in, states, base, late
    )
    new_key = key_rows.reshape(requests, span, needed)
    if own_width != needed:
        new_key = lax.dynamic_slice_in_dim(
            new_key, position * own_width - column_start, own_width, 2
        )
    new_value = value_rows.reshape(requests, span, heads * size)
    return (mixed, new_states, new_key, new_value)


def solution(mesh):
    in_specs = (
        P("req", None, "head"),
        P("head", None),
        P(None, "head", None),
        P(None, "head", None),
        P(),
        P(None, "head"),
        P("req", None, None),
        P("req", None, "head"),
        P("req", "head", None, None),
        P("head"),
        P("head"),
        P(),
        P("head", None),
        P("req"),
        P("req"),
        P("req"),
    )
    out_specs = (
        P("req", None, "head"),
        P("req", "head", None, None),
        P("req", None, "head"),
        P("req", None, "head"),
    )
    return jax.shard_map(local, mesh=mesh, in_specs=in_specs, out_specs=out_specs, check_vma=False)
```

time: 565 us -> 250 us (0.44)
  the two profiles are of different devices: /device:TPU:0 before, /device:TPU:16 now
where the time goes in v1:
time: 250 us; the launch traced here: 255 us
  blocking collectives  112 us (45%)
  Pallas kernels  56.5 us (23%)
  local copies, waits for them, and re-layouts  31.1 us (12%)
  starting transfers between devices  18.3 us (7%)
  between operations  16.2 us (6%)
  waiting for transfers between devices  12.5 us (5%)
  other arithmetic  6.13 us (2%)
    all_gather x1, blocking collectives, local(): plan = lax.all_gather(jnp.stack([next_group, next_slot]), 'req', axis=0)  91.8 us
    pallas_call x2, Pallas kernels, pack(): pl.pallas_call(pack_kernel, out_shape=jax.ShapeDtypeStruct((count,) + sta...  23.1 us
    pallas_call x1, Pallas kernels, place(): pl.pallas_call(functools.partial(place_kernel, dims), out_shape=(jax.Shap...  22.9 us
    all_gather x1, blocking collectives, local(): lax.all_gather(jnp.swapaxes(hidden, 0, 1).reshape(rows, feature_piece), '...  20.7 us
    unnamed x50, local copies, waits for them, and re-layouts  16.8 us
    ppermute x1, waiting for transfers between devices, send(): return lax.ppermute(pack(source_states, rows_out), 'req', pairs)  11.6 us
    pallas_call x1, Pallas kernels, verify(): pl.pallas_call(functools.partial(verify_kernel, dims), out_shape=(jax.Sha...  10.5 us
    all_to_all x1, starting transfers between devices, local(): lax.all_to_all(base_send, 'req', split_axis=0, concat_axis=0, tiled=True)  8.08 us
  transfers between devices with their start and end apart: 5, of which 2 were waited for; matrix products, arithmetic and copies ran while one was open for 8% of the time, Pallas kernels for 9%

profile of v1, /device:TPU:16, one launch (start us, length us, event | category | flops | bytes accessed | tf_op | source)
XLA Modules:
  0.0 254.9 jit_solution(15791703092554627381)
XLA Ops:
  7.2 3.2 %copy.47 = bf16[32,8,8,512]{3,2,0,1:T(8,128)(2,1)} copy(bf16[32,8,8,512]{3,2,1,0:T(8,128)(2,1)} %bitcast.50) | data formatting | bytes 4194304 | tf_op jit(solution)/shard_map/all_to_all | solution.py:410
  10.5 4.5 %all-to-all-start = ((bf16[256,8,512]{2,0,1:T(8,128)(2,1)}), bf16[256,8,512]{2,0,1:T(8,128)(2,1)}, u32[]{:S(2)}, u32[]{:S(2)}) async-start(bf16[256,8,512]{2,0,1:T(8,128)(2,1)} %bitcast.48), calls=%async_computation | async-start | bytes 4194304 | tf_op jit(solution)/shard_map/all_to_all | solution.py:410
  18.2 5.3 %copy.43 = bf16[256,8,4,256]{3,1,2,0:T(8,128)(2,1)} copy(bf16[256,8,4,256]{3,2,1,0:T(4,128)(2,1)} %bitcast.49) | data formatting | bytes 8388608
  23.5 1.3 constant_dynamic-slice_fusion.ck_ref
  24.8 0.9 dynamic-slice_bitcast_fusion.3.ks_ref
  25.7 20.7 %all_gather.9.x_ref = bf16[8,160,256]{2,1,0:T(8,128)(2,1)S(1)} all-gather(bf16[1,160,256]{2,1,0:T(8,128)(2,1)S(1)} %bitcast.52), channel_id=1, replica_groups=mesh['head'=8,'req'=4] {'head'}, dimensions={0}, use_global_device_ids=true | all-gather | bytes 737280 | tf_op jit(solution)/shard_map/all_gather | solution.py:408
  46.4 2.2 copy-done.1
  48.6 0.9 copy-done.4
  49.5 0.7 copy-done.5
  53.4 10.5 %verify_window.1 = (bf16[160,512]{1,0:T(8,128)(2,1)S(1)}, bf16[48,7424]{1,0:T(8,128)(2,1)S(1)}) custom-call(bf16[8,160,256]{2,1,0:T(8,128)(2,1)S(1)} %all_gather.9.x_ref, bf16[2048,512]{1,0:T(8,128)(2,1)} %bitcast.6.wk_ref, bf16[2048,1024]{1,0:T(8,128)(2,1)S(1)} %bitcast.43, bf16[2048,8]{1,0:T(8,128)(2,1)S(1)} %copy.36.wg_ref, bf16[4,512]{1,0:T(4,128)(2,1)S(1)} %copy-done.6, ...), custom_call_target="tpu_custom_call" | custom-call | tf_op jit(solution)/shard_map/verify_window/pallas_call | solution.py:226
  63.9 0.8 copy-done.3
  64.7 2.2 all_to_all.28
  67.0 5.2 %all-to-all-start.1 = ((bf16[4,12,7424]{2,1,0:T(8,128)(2,1)}), bf16[4,12,7424]{2,1,0:T(8,128)(2,1)S(1)}, u32[]{:S(2)}, u32[]{:S(2)}) async-start(bf16[4,12,7424]{2,1,0:T(8,128)(2,1)} %all_to_all.28), calls=%async_computation.2 | async-start | bytes 1900544 | tf_op jit(solution)/shard_map/all_to_all | solution.py:437
  72.9 19.2 %pack_states.7 = bf16[32,4,128,128]{3,2,1,0:T(8,128)(2,1)} custom-call(s32[32]{0:T(128)} %reshape.117.index_ref, f32[32,4,128,128]{3,2,1,0:T(8,128)} %st_ref.3), custom_call_target="tpu_custom_call" | custom-call | tf_op jit(solution)/shard_map/pack_states/pallas_call | solution.py:36
  92.1 0.9 all-to-all-done.1
  93.0 0.9 copy-done.11
  94.0 8.1 %all-to-all-start.2 = ((bf16[32,4,128,128]{3,2,1,0:T(8,128)(2,1)}), bf16[32,4,128,128]{3,2,1,0:T(8,128)(2,1)}, u32[]{:S(2)}, u32[]{:S(2)}) async-start(bf16[32,4,128,128]{3,2,1,0:T(8,128)(2,1)} %pack_states.7), calls=%async_computation.3 | async-start | bytes 8388608 | tf_op jit(solution)/shard_map/all_to_all | solution.py:406
  102.1 1.6 fusion.10
  103.8 91.8 %all-gather.1 = s32[4,2,32]{2,1,0:T(2,128)S(1)} all-gather(s32[1,2,32]{2,1,0:T(2,128)S(1)} %add_bitcast_fusion), channel_id=2, replica_groups=mesh['head'=8,'req'=4] {'req'}, dimensions={0}, use_global_device_ids=true | all-gather | bytes 1280 | tf_op jit(solution)/shard_map/all_gather | solution.py:411
  196.2 0.7 select_reduce_fusion.6
  199.0 0.9 conditional.5
  199.0 0.9 broadcast.99
  199.9 1.0 conditional.4
  199.9 1.0 broadcast.98
  200.8 16.5 %conditional.3 = (bf16[4,4,128,128]{3,2,1,0:T(8,128)(2,1)}) conditional(s32[]{:T(128)} %convert_element_type.49, () %tuple.28, (s32[]{:T(128)}, s32[4,4]{1,0:T(4,128)S(1)}, f32[32,4,128,128]{3,2,1,0:T(8,128)}) %tuple.29), branch_computations={%region_10.11_spmd, %region_11.12_spmd} | conditional | flops 15 | bytes 2097391 | solution.py:481
  201.3 3.9 %pack_states.4 = bf16[4,4,128,128]{3,2,1,0:T(8,128)(2,1)} custom-call(s32[4]{0:T(128)} %dynamic-slice_bitcast_fusion.index_ref, f32[32,4,128,128]{3,2,1,0:T(8,128)} %get-tuple-element.25.in_ref), custom_call_target="tpu_custom_call" | custom-call | tf_op jit(solution)/shard_map/cond/branch_1_fun/pack_states/pallas_call | solution.py:36
  205.8 11.6 %collective-permute-done = bf16[4,4,128,128]{3,2,1,0:T(8,128)(2,1)} collective-permute-done((bf16[4,4,128,128]{3,2,1,0:T(8,128)(2,1)}, bf16[4,4,128,128]{3,2,1,0:T(8,128)(2,1)}, u32[]{:S(2)}, u32[]{:S(2)}) %collective-permute-start) | collective-permute-done | bytes 524320 | tf_op jit(solution)/shard_map/cond/branch_1_fun/ppermute | solution.py:475
  217.3 2.7 %pad_maximum_fusion.extra_ref = bf16[12,4,128,128]{3,2,1,0:T(8,128)(2,1)} fusion(bf16[4,4,128,128]{3,2,1,0:T(8,128)(2,1)} %get-tuple-element.89, bf16[4,4,128,128]{3,2,1,0:T(8,128)(2,1)} %get-tuple-element.88, bf16[4,4,128,128]{3,2,1,0:T(8,128)(2,1)} %get-tuple-element.87), kind=kLoop, calls=%fused_computation.4 | loop fusion | flops 1572864 | bytes 3145728 | tf_op jit(solution)/shard_map/concatenate | solution.py:484
  220.0 1.4 all_to_all.30.pay_ref
  221.4 1.6 convert_element_type.45
  223.0 1.4 copy-done.2
  224.4 22.9 %place_states.1 = (f32[32,4,128,128]{3,2,1,0:T(8,128)}, bf16[32,1536]{1,0:T(8,128)(2,1)S(1)}, bf16[32,1536]{1,0:T(8,128)(2,1)S(1)}) custom-call(s32[32]{0:T(128)S(1)} %get-tuple-element.77.kind_ref, s32[32]{0:T(128)S(1)} %get-tuple-element.84.own_index, s32[32]{0:T(128)S(1)} %get-tuple-element.83.base_index, s32[32]{0:T(128)S(1)} %get-tuple-element.76.extra_index, ...), custom_call_target="tpu_custom_call" | custom-call | tf_op jit(solution)/shard_map/place_states/pallas_call | solution.py:327
  (77 shorter events, 9.7 us)
Async XLA Ops:
  7.2 94.9 %copy-start = (bf16[512,2048]{1,0:T(8,128)(2,1)S(1)}, bf16[512,2048]{1,0:T(8,128)(2,1)}, u32[]{:S(2)}) copy-start(bf16[512,2048]{1,0:T(8,128)(2,1)} %param.34) | copy-start | bytes 6291460
  10.4 4.5 %copy-start.20 = (f32[4]{0:T(128)S(1)}, f32[4]{0:T(128)}, u32[]{:S(2)}) copy-start(f32[4]{0:T(128)} %param.31) | copy-start | bytes 52
  10.4 5.2 %copy-start.21 = (f32[4]{0:T(128)S(1)}, f32[4]{0:T(128)}, u32[]{:S(2)}) copy-start(f32[4]{0:T(128)} %param.32) | copy-start | bytes 52
  10.4 5.9 %copy-start.22 = (s32[32]{0:T(128)S(1)}, s32[32]{0:T(128)}, u32[]{:S(2)}) copy-start(s32[32]{0:T(128)} %param.35) | copy-start | bytes 388
  10.4 5.9 %copy-start.16 = (s32[32]{0:T(128)S(1)}, s32[32]{0:T(128)}, u32[]{:S(2)}) copy-start(s32[32]{0:T(128)} %param.36) | copy-start | bytes 388
  10.4 7.5 %copy-start.13 = (bf16[2048,4,2]{0,2,1:T(2,128)(2,1)S(1)}, bf16[2048,4,2]{0,2,1:T(2,128)(2,1)}, u32[]{:S(2)}) copy-start(bf16[2048,4,2]{0,2,1:T(2,128)(2,1)} %param.25) | copy-start | bytes 98308
  10.5 35.9 %all-to-all-start = ((bf16[256,8,512]{2,0,1:T(8,128)(2,1)}), bf16[256,8,512]{2,0,1:T(8,128)(2,1)}, u32[]{:S(2)}, u32[]{:S(2)}) async-start(bf16[256,8,512]{2,0,1:T(8,128)(2,1)} %bitcast.48), calls=%async_computation | async-start | bytes 4194304 | tf_op jit(solution)/shard_map/all_to_all | solution.py:410
  16.7 0.6 copy-start.18
  16.7 0.6 copy-start.14
  18.2 7.5 %copy-start.12 = (bf16[32,5,256]{2,0,1:T(8,128)(2,1)S(1)}, bf16[32,5,256]{2,0,1:T(8,128)(2,1)}, u32[]{:S(2)}) copy-start(bf16[32,5,256]{2,0,1:T(8,128)(2,1)} %param.22) | copy-start | bytes 245764
  46.4 2.2 copy-start.1
  48.6 0.9 copy-start.4
  49.5 0.7 copy-start.5
  50.2 0.7 copy-start.6
  50.9 0.7 copy-start.7
  51.6 0.6 copy-start.8
  52.1 0.6 copy-start.9
  52.7 0.7 copy-start.10
  63.9 0.9 copy-start.3
  64.7 7.4 %copy-start.15 = (pred[12,32]{1,0:T(8,128)(4,1)S(1)}, pred[12,32]{1,0:T(8,128)(4,1)}, u32[]{:S(2)}) copy-start(pred[12,32]{1,0:T(8,128)(4,1)} %copy-done.14) | copy-start | bytes 1156
  64.7 7.4 %copy-start.19 = (pred[4,32]{1,0:T(4,128)(4,1)S(1)}, pred[4,32]{1,0:T(4,128)(4,1)}, u32[]{:S(2)}) copy-start(pred[4,32]{1,0:T(4,128)(4,1)} %copy-done.18) | copy-start | bytes 388
  67.0 26.1 %all-to-all-start.1 = ((bf16[4,12,7424]{2,1,0:T(8,128)(2,1)}), bf16[4,12,7424]{2,1,0:T(8,128)(2,1)S(1)}, u32[]{:S(2)}, u32[]{:S(2)}) async-start(bf16[4,12,7424]{2,1,0:T(8,128)(2,1)} %all_to_all.28), calls=%async_computation.2 | async-start | bytes 1900544 | tf_op jit(solution)/shard_map/all_to_all | solution.py:437
  93.0 0.9 copy-start.11
  94.0 129.0 %all-to-all-start.2 = ((bf16[32,4,128,128]{3,2,1,0:T(8,128)(2,1)}), bf16[32,4,128,128]{3,2,1,0:T(8,128)(2,1)}, u32[]{:S(2)}, u32[]{:S(2)}) async-start(bf16[32,4,128,128]{3,2,1,0:T(8,128)(2,1)} %pack_states.7), calls=%async_computation.3 | async-start | bytes 8388608 | tf_op jit(solution)/shard_map/all_to_all | solution.py:406
  102.1 119.4 %reduce-scatter.2.cloned.1.call-start = ((), (), s32[]{:S(2)}) async-start(), calls=%async_computation.4 | async-start | bytes 1474560 | tf_op jit(solution)/shard_map/reduce_scatter | solution.py:435
  102.1 1.7 copy-start.17
  102.1 1.7 copy-start.23
  205.2 12.1 %collective-permute-start = (bf16[4,4,128,128]{3,2,1,0:T(8,128)(2,1)}, bf16[4,4,128,128]{3,2,1,0:T(8,128)(2,1)}, u32[]{:S(2)}, u32[]{:S(2)}) collective-permute-start(bf16[4,4,128,128]{3,2,1,0:T(8,128)(2,1)} %pack_states.4), channel_id=1, source_target_pairs={{0,1},{1,2},{2,3},{3,0},{4,5},{5,6},{6,7},{7,4},{8,9},{9,10},{10,1... | collective-permute-start | bytes 1572872 | tf_op jit(solution)/shard_map/cond/branch_1_fun/ppermute | solution.py:475
  223.0 1.4 copy-start.2
Sparse Core Ops, SparseCore 0:
  106.1 37.1 reduce-scatter.1

commit v2 on v1

--- a/solution.py
+++ b/solution.py
@@ -6,6 +6,7 @@
 from jax.experimental import pallas as pl
 from jax.experimental.pallas import tpu as pltpu
 from jax.sharding import PartitionSpec as P
+
 
 CAP = 12
 F32 = jnp.float32
@@ -25,25 +26,31 @@
     return x / (1.0 + jnp.exp(-x))
 
 
-def pack_kernel(index_ref, in_ref, out_ref):
-    out_ref[...] = in_ref[...].astype(out_ref.dtype)
+def pack_kernel(index_ref, *refs):
+    out_ref = refs[-1]
+    for row, in_ref in enumerate(refs[:-1]):
+        out_ref[row] = in_ref[0].astype(out_ref.dtype)
 
 
 def pack(states, picked):
     count = picked.shape[0]
-    block = (1,) + states.shape[1:]
-    zeros = (0,) * (states.ndim - 1)
+    batch = 4 if count % 4 == 0 else 1
+    block = states.shape[1:]
+    zeros = (0,) * len(block)
     return pl.pallas_call(
         pack_kernel,
-        out_shape=jax.ShapeDtypeStruct((count,) + states.shape[1:], BF16),
+        out_shape=jax.ShapeDtypeStruct((count,) + block, BF16),
         grid_spec=pltpu.PrefetchScalarGridSpec(
             num_scalar_prefetch=1,
-            grid=(count,),
-            in_specs=[pl.BlockSpec(block, lambda i, index: (index[i],) + zeros)],
-            out_specs=pl.BlockSpec(block, lambda i, index: (i,) + zeros),
+            grid=(count // batch,),
+            in_specs=[
+                pl.BlockSpec((1,) + block, lambda i, index, j=j: (index[i * batch + j],) + zeros)
+                for j in range(batch)
+            ],
+            out_specs=pl.BlockSpec((batch,) + block, lambda i, index: (i,) + zeros),
         ),
         name="pack_states",
-    )(picked, states)
+    )(picked, *([states] * batch))
 
 
 def layout(key_heads, heads, window, span, size, needed):
@@ -70,6 +77,7 @@
     nw_ref,
     acc_ref,
     oh_ref,
+    plan_ref,
     st_ref,
     normed_ref,
     pay_ref,
@@ -209,14 +217,19 @@
                     p_s[:, at : at + size] = (kept_coef[j] * deltas[j]).astype(BF16)
                 at = o_scale + h * size
                 p_s[:, at : at + size] = jnp.broadcast_to(kept_whole, (requests, size)).astype(BF16)
-        pay_ref[...] = jnp.dot(oh_ref[...], p_s[...], preferred_element_type=F32).astype(BF16)
-
-
-def verify(dims, x, wk, wv, wg, ck, cv, ks, vs, al, db, nw, acc, oh, states):
+        width = p_s.shape[1]
+        pay_ref[:, :width] = jnp.dot(oh_ref[...], p_s[...], preferred_element_type=F32).astype(BF16)
+        pay_ref[:, width:] = jnp.broadcast_to(
+            plan_ref[...], (pay_ref.shape[0], plan_ref.shape[1])
+        ).astype(BF16)
+
+
+def verify(dims, x, wk, wv, wg, ck, cv, ks, vs, al, db, nw, acc, oh, plan, states):
     requests, window, heads, key_heads, size, span, needed, batch, slots = dims
     rows = requests * window
     width = layout(key_heads, heads, window, span, size, needed)[-1]
-    small = [x, wk, wv, wg, ck, cv, ks, vs, al, db, nw, acc, oh]
+    small = [x, wk, wv, wg, ck, cv, ks, vs, al, db, nw, acc, oh, plan]
+    sent = width + plan.shape[1]
 
     def whole(shape):
         return pl.BlockSpec(
@@ -227,14 +240,14 @@
         functools.partial(verify_kernel, dims),
         out_shape=(
             jax.ShapeDtypeStruct((rows, heads * size), BF16),
-            jax.ShapeDtypeStruct((oh.shape[0], width), BF16),
+            jax.ShapeDtypeStruct((oh.shape[0], sent), BF16),
         ),
         grid=(requests // batch,),
         in_specs=[whole(a.shape) for a in small]
         + [pl.BlockSpec((batch,) + states.shape[1:], lambda i: (i, 0, 0, 0))],
         out_specs=(
             pl.BlockSpec((rows, heads * size), lambda i: (0, 0)),
-            pl.BlockSpec((oh.shape[0], width), lambda i: (0, 0)),
+            pl.BlockSpec((oh.shape[0], sent), lambda i: (0, 0)),
         ),
         scratch_shapes=[
             pltpu.VMEM((key_heads, requests * slots, size), F32),
@@ -250,25 +263,12 @@
     )(*small, states)
 
 
-def place_kernel(
-    dims,
-    kind_ref,
-    own_index,
-    base_index,
-    extra_index,
-    oh_ref,
-    pay_ref,
-    st_ref,
-    base_ref,
-    extra_ref,
-    out_ref,
-    kt_ref,
-    vt_ref,
-    k_s,
-    d_s,
-    w_s,
-):
-    requests, window, heads, key_heads, size, span, needed, lines = dims
+def place_kernel(dims, count, kind_ref, *refs):
+    requests, window, heads, key_heads, size, span, needed, lines, batch = dims
+    refs = refs[count:]
+    oh_ref, pay_ref = refs[:2]
+    sources = refs[2 : 2 + count * batch]
+    out_ref, kt_ref, vt_ref, k_s, d_s, w_s = refs[2 + count * batch :]
     ratio = heads // key_heads
     o_key, o_delta, o_scale, o_kt, o_vt, width = layout(
         key_heads, heads, window, span, size, needed
@@ -296,28 +296,31 @@
         kt_ref[...] = columns(o_kt, o_vt).astype(BF16)
         vt_ref[...] = columns(o_vt, width).astype(BF16)
 
-    def apply(source_ref):
-        row = pl.multiple_of(step * lines, lines)
+    def apply(slot, source_ref):
+        index = step * batch + slot
+        row = pl.multiple_of(index * lines, lines)
         for h in range(heads):
             k = k_s[h // ratio, pl.ds(row, lines), :].astype(BF16)
             d = d_s[h, pl.ds(row, lines), :].astype(BF16)
             update = lax.dot_general(
                 k, d, (((0,), (0,)), ((), ())), preferred_element_type=F32
             )
-            weight = w_s[h, pl.ds(step, 1), :]
-            out_ref[0, h] = weight * source_ref[0, h].astype(F32) + update
-
-    kind = kind_ref[step]
-    for value, source_ref in enumerate((st_ref, base_ref, extra_ref)):
-
-        @pl.when(kind == value)
-        def _(source_ref=source_ref):
-            apply(source_ref)
-
-
-def place(dims, kind, own_i, base_i, extra_i, oh, pay, states, base, extra):
-    requests, window, heads, key_heads, size, span, needed, lines = dims
-    block = (1,) + states.shape[1:]
+            weight = w_s[h, pl.ds(index, 1), :]
+            out_ref[slot, h] = weight * source_ref[0, h].astype(F32) + update
+
+    for slot in range(batch):
+        kind = kind_ref[step * batch + slot]
+        for value in range(count):
+
+            @pl.when(kind == value)
+            def _(slot=slot, source_ref=sources[value * batch + slot]):
+                apply(slot, source_ref)
+
+
+def place(dims, kind, indexes, oh, pay, sources):
+    requests, _, heads, key_heads, size, span, needed, lines, batch = dims
+    block = sources[0].shape[1:]
+    count = len(sources)
 
     def whole(shape):
         return pl.BlockSpec(
@@ -325,24 +328,26 @@
         )
 
     return pl.pallas_call(
-        functools.partial(place_kernel, dims),
+        functools.partial(place_kernel, dims, count),
         out_shape=(
-            jax.ShapeDtypeStruct(states.shape, F32),
+            jax.ShapeDtypeStruct((requests,) + block, F32),
             jax.ShapeDtypeStruct((requests, span * needed), BF16),
             jax.ShapeDtypeStruct((requests, span * heads * size), BF16),
         ),
         grid_spec=pltpu.PrefetchScalarGridSpec(
-            num_scalar_prefetch=4,
-            grid=(requests,),
-            in_specs=[
-                whole(oh.shape),
-                whole(pay.shape),
-                pl.BlockSpec(block, lambda i, kind, a, b, c: (a[i], 0, 0, 0)),
-                pl.BlockSpec(block, lambda i, kind, a, b, c: (b[i], 0, 0, 0)),
-                pl.BlockSpec(block, lambda i, kind, a, b, c: (c[i], 0, 0, 0)),
+            num_scalar_prefetch=1 + count,
+            grid=(requests // batch,),
+            in_specs=[whole(oh.shape), whole(pay.shape)]
+            + [
+                pl.BlockSpec(
+                    (1,) + block,
+                    lambda i, kind, *index, v=v, j=j: (index[v][i * batch + j], 0, 0, 0),
+                )
+                for v in range(count)
+                for j in range(batch)
             ],
             out_specs=(
-                pl.BlockSpec(block, lambda i, *_: (i, 0, 0, 0)),
+                pl.BlockSpec((batch,) + block, lambda i, *_: (i, 0, 0, 0)),
                 pl.BlockSpec((requests, span * needed), lambda i, *_: (0, 0)),
                 pl.BlockSpec((requests, span * heads * size), lambda i, *_: (0, 0)),
             ),
@@ -352,9 +357,9 @@
                 pltpu.VMEM((heads, requests, size), F32),
             ],
         ),
-        compiler_params=pltpu.CompilerParams(vmem_limit_bytes=32 * 1024 * 1024),
+        compiler_params=pltpu.CompilerParams(vmem_limit_bytes=40 * 1024 * 1024),
         name="place_states",
-    )(kind, own_i, base_i, extra_i, oh, pay, states, base, extra)
+    )(kind, *indexes, oh, pay, *[source for source in sources for _ in range(batch)])
 
 
 def local(
@@ -402,13 +407,31 @@
         matched.astype(jnp.int32) * jnp.arange(requests, dtype=jnp.int32)[None, None, :], axis=2
     )
 
-    base_send = pack(states, picked[:, :share].reshape(-1))
-    base = lax.all_to_all(base_send, "req", split_axis=0, concat_axis=0, tiled=True)
-
-    gathered = lax.all_gather(jnp.swapaxes(hidden, 0, 1).reshape(rows, feature_piece), "head", axis=0)
+    moves = {}
+    for shift in range(1, groups):
+        moves[shift] = [(s, (s + shift) % groups) for s in range(groups)]
+    order = sorted(moves, key=lambda shift: (abs(2 * shift - groups), shift))
+    sends = {}
+    for shift in order:
+        rows_out = lax.dynamic_index_in_dim(
+            picked[:, :share], (group + shift) % groups, 0, keepdims=False
+        )
+        sends[shift] = pack(states, rows_out)
+    sends, hidden, w_key, w_value, w_gates, key_conv_state, value_conv_state = (
+        lax.optimization_barrier(
+            (sends, hidden, w_key, w_value, w_gates, key_conv_state, value_conv_state)
+        )
+    )
+    base = {}
+    for shift in order:
+        base[shift] = lax.ppermute(sends[shift], "req", moves[shift])
+
+    own_rows = jnp.swapaxes(hidden, 0, 1).reshape(rows, feature_piece)
+    gathered = lax.all_gather(own_rows, "head", axis=0)
     spread = spread_heads(w_key, devices, key_heads, pair_width)
     columns = lax.all_to_all(spread, "head", split_axis=1, concat_axis=0, tiled=True)
-    plan = lax.all_gather(jnp.stack([next_group, next_slot]), "req", axis=0)
+    own_plan = jnp.concatenate([next_group, next_slot]).astype(F32)
+    own_plan = jnp.pad(own_plan, (0, -own_plan.shape[0] % 128))[None, :]
 
     local_state = lax.dynamic_slice_in_dim(key_conv_state, column_start, needed, 2)
     local_taps = lax.dynamic_slice_in_dim(conv_key, column_start, needed, 1)
@@ -429,12 +452,16 @@
         norm_weight[None, :],
         accepted[:, None],
         send_rows,
+        own_plan,
         states,
     )
     partial_out = jnp.dot(normed, w_out, preferred_element_type=F32)
     mixed = lax.psum_scatter(partial_out, "head", scatter_dimension=1, tiled=True).astype(BF16)
     mixed = jnp.swapaxes(mixed.reshape(window, requests, -1), 0, 1)
     pay_in = lax.all_to_all(pay, "req", split_axis=0, concat_axis=0, tiled=True)
+    plan_at = pay.shape[1] - own_plan.shape[1]
+    plan = pay_in[::CAP, plan_at : plan_at + 2 * requests].astype(jnp.int32)
+    plan = plan.reshape(groups, 2, requests)
 
     groups_of, slots_of = plan[:, 0], plan[:, 1]
     mine = (groups_of == group).astype(jnp.int32)
@@ -446,8 +473,9 @@
     origin = jnp.sum(hit * jnp.arange(requests, dtype=jnp.int32)[None, None, :], axis=(1, 2))
     row_of = source * CAP + place_rank
     take_rows = (row_of[:, None] == jnp.arange(groups * CAP, dtype=jnp.int32)[None, :]).astype(BF16)
-    kind = jnp.where(source == group, 0, jnp.where(place_rank < share, 1, 2)).astype(jnp.int32)
     shift_in = (group - source + groups) % groups
+    kind = jnp.where(shift_in == 0, 0, jnp.where(place_rank < share, shift_in, groups - 1 + shift_in))
+    kind = kind.astype(jnp.int32)
 
     counts = jnp.sum(
         (groups_of[:, None, :] == jnp.arange(groups, dtype=jnp.int32)[None, :, None]).astype(
@@ -463,14 +491,11 @@
     extra_block = (max(extra, 1),) + states.shape[1:]
     late = []
     pick_extra = picked[:, share:]
-    pick_extra, counts, partial_out, pay = lax.optimization_barrier(
-        (pick_extra, counts, partial_out, pay)
-    )
+    pick_extra, counts, _ = lax.optimization_barrier((pick_extra, counts, partial_out))
     for shift in range(1, groups):
         most = jnp.max(jnp.where(shifts == shift, counts, 0))
-        pairs = [(s, (s + shift) % groups) for s in range(groups)]
-
-        def send(pick, source_states, pairs=pairs, shift=shift):
+
+        def send(pick, source_states, pairs=moves[shift], shift=shift):
             rows_out = lax.dynamic_index_in_dim(pick, (group + shift) % groups, 0, keepdims=False)
             return lax.ppermute(pack(source_states, rows_out), "req", pairs)
 
@@ -481,16 +506,27 @@
             late.append(lax.cond(most > share, send, skip, pick_extra, states))
         else:
             late.append(jnp.zeros(extra_block, BF16))
-    late = jnp.concatenate(late, axis=0)
-
-    own_i = jnp.where(kind == 0, origin, 0).astype(jnp.int32)
-    base_i = jnp.where(kind == 1, source * share + place_rank, 0).astype(jnp.int32)
-    extra_i = jnp.where(
-        kind == 2, (shift_in - 1) * extra_block[0] + place_rank - share, 0
+
+    batch = 4 if requests % 4 == 0 else 1
+    wanted = jnp.where(
+        kind == 0,
+        origin,
+        jnp.where(kind < groups, place_rank, place_rank - share),
     ).astype(jnp.int32)
-    dims = (requests, window, heads, key_heads, size, span, needed, 8)
+    limit = max(requests, groups * CAP)
+    turn = jnp.arange(requests, dtype=jnp.int32) // batch
+    used = kind[None, :] == jnp.arange(2 * groups - 1, dtype=jnp.int32)[:, None]
+    coded = jnp.where(used, (turn * limit + wanted)[None, :], 0)
+    coded = lax.cummax(coded.reshape(2 * groups - 1, requests // batch, batch), axis=1)
+    indexes = lax.rem(coded, limit).reshape(2 * groups - 1, requests)
+    dims = (requests, window, heads, key_heads, size, span, needed, 8, batch)
     new_states, key_rows, value_rows = place(
-        dims, kind, own_i, base_i, extra_i, take_rows, pay_in, states, base, late
+        dims,
+        kind,
+        [indexes[v] for v in range(2 * groups - 1)],
+        take_rows,
+        pay_in,
+        [states] + [base[shift] for shift in range(1, groups)] + late,
     )
     new_key = key_rows.reshape(requests, span, needed)
     if own_width != needed:
@@ -526,4 +562,5 @@
         P("req", None, "head"),
         P("req", None, "head"),
     )
+
     return jax.shard_map(local, mesh=mesh, in_specs=in_specs, out_specs=out_specs, check_vma=False)

time: 250 us -> 221 us (0.88)
  the two profiles are of different devices: /device:TPU:16 before, /device:TPU:8 now
where the time goes in v2:
time: 221 us; the launch traced here: 220 us
  waiting for transfers between devices  97 us (44%)
  Pallas kernels  35.7 us (16%)
  local copies, waits for them, and re-layouts  26 us (12%)
  blocking collectives  23.7 us (11%)
  between operations  16.2 us (7%)
  starting transfers between devices  14.2 us (6%)
  other arithmetic  5.64 us (3%)
    ppermute x3, waiting for transfers between devices, local(): base[shift] = lax.ppermute(sends[shift], 'req', moves[shift])  80.9 us
    all_gather x1, blocking collectives, local(): gathered = lax.all_gather(own_rows, 'head', axis=0)  23.7 us
    pallas_call x1, Pallas kernels, place(): pl.pallas_call(functools.partial(place_kernel, dims, count), out_shape=(j...  16.1 us
    all_to_all x1, waiting for transfers between devices, local(): pay_in = lax.all_to_all(pay, 'req', split_axis=0, concat_axis=0, tiled=True)  16.1 us
    unnamed x32, local copies, waits for them, and re-layouts  11.5 us
    pallas_call x1, Pallas kernels, verify(): pl.pallas_call(functools.partial(verify_kernel, dims), out_shape=(jax.Sha...  10.5 us
    pallas_call x3, Pallas kernels, pack(): pl.pallas_call(pack_kernel, out_shape=jax.ShapeDtypeStruct((count,) + blo...  9.17 us
    all_to_all x1, starting transfers between devices, local(): pay_in = lax.all_to_all(pay, 'req', split_axis=0, concat_axis=0, tiled=True)  5.31 us
  transfers between devices with their start and end apart: 6, of which 4 were waited for; matrix products, arithmetic and copies ran while one was open for 8% of the time, Pallas kernels for 7%

profile of v2, /device:TPU:8, one launch (start us, length us, event | category | flops | bytes accessed | tf_op | source)
XLA Modules:
  0.0 220.0 jit_solution(8280431227909848520)
XLA Ops:
  10.4 3.1 %pack_states.11 = bf16[8,4,128,128]{3,2,1,0:T(8,128)(2,1)} custom-call(s32[8]{0:T(128)} %get-tuple-element.109.index_ref, f32[32,4,128,128]{3,2,1,0:T(8,128)} %refs_12_.1, f32[32,4,128,128]{3,2,1,0:T(8,128)} %refs_12_.1, f32[32,4,128,128]{3,2,1,0:T(8,128)} %refs_12_.1, f32[32,4,128,128]{3,2,1,0:T(8,128)} %refs_12_.1), custom_call_target="tpu_custom_call" | custom-call | tf_op jit(solution)/shard_map/pack_states/pallas_call | solution.py:40
  13.4 3.0 %pack_states.10 = bf16[8,4,128,128]{3,2,1,0:T(8,128)(2,1)} custom-call(s32[8]{0:T(128)} %get-tuple-element.110.index_ref, f32[32,4,128,128]{3,2,1,0:T(8,128)} %refs_12_.1, f32[32,4,128,128]{3,2,1,0:T(8,128)} %refs_12_.1, f32[32,4,128,128]{3,2,1,0:T(8,128)} %refs_12_.1, f32[32,4,128,128]{3,2,1,0:T(8,128)} %refs_12_.1), custom_call_target="tpu_custom_call" | custom-call | tf_op jit(solution)/shard_map/pack_states/pallas_call | solution.py:40
  16.5 3.1 %pack_states.9 = bf16[8,4,128,128]{3,2,1,0:T(8,128)(2,1)} custom-call(s32[8]{0:T(128)} %get-tuple-element.111.index_ref, f32[32,4,128,128]{3,2,1,0:T(8,128)} %refs_12_.1, f32[32,4,128,128]{3,2,1,0:T(8,128)} %refs_12_.1, f32[32,4,128,128]{3,2,1,0:T(8,128)} %refs_12_.1, f32[32,4,128,128]{3,2,1,0:T(8,128)} %refs_12_.1), custom_call_target="tpu_custom_call" | custom-call | tf_op jit(solution)/shard_map/pack_states/pallas_call | solution.py:40
  19.5 3.2 %copy.57 = bf16[32,8,8,512]{3,2,0,1:T(8,128)(2,1)} copy(bf16[32,8,8,512]{3,2,1,0:T(8,128)(2,1)} %bitcast.58) | data formatting | bytes 4194304 | tf_op jit(solution)/shard_map/all_to_all | solution.py:432
  22.7 4.5 %all-to-all-start = ((bf16[256,8,512]{2,0,1:T(8,128)(2,1)}), bf16[256,8,512]{2,0,1:T(8,128)(2,1)}, u32[]{:S(2)}, u32[]{:S(2)}) async-start(bf16[256,8,512]{2,0,1:T(8,128)(2,1)} %bitcast.56), calls=%async_computation | async-start | bytes 4194304 | tf_op jit(solution)/shard_map/all_to_all | solution.py:432
  27.7 1.0 copy.42.wg_ref
  28.7 5.3 %copy.53 = bf16[256,8,4,256]{3,1,2,0:T(8,128)(2,1)} copy(bf16[256,8,4,256]{3,2,1,0:T(4,128)(2,1)} %bitcast.57) | data formatting | bytes 8388608
  34.8 0.9 dynamic-slice_bitcast_fusion.3.ks_ref
  35.7 23.7 %all_gather.3.x_ref = bf16[8,160,256]{2,1,0:T(8,128)(2,1)} all-gather(bf16[1,160,256]{2,1,0:T(8,128)(2,1)S(1)} %bitcast.60), channel_id=1, replica_groups=mesh['head'=8,'req'=4] {'head'}, dimensions={0}, use_global_device_ids=true | all-gather | bytes 737280 | tf_op jit(solution)/shard_map/all_gather | solution.py:430
  59.4 2.2 copy-done.1
  61.6 1.1 copy-done.3
  62.7 1.0 copy-done.4
  63.7 10.5 %verify_window.1 = (bf16[160,512]{1,0:T(8,128)(2,1)S(1)}, bf16[48,7552]{1,0:T(8,128)(2,1)S(1)}) custom-call(bf16[8,160,256]{2,1,0:T(8,128)(2,1)S(1)} %copy-done.3, bf16[2048,512]{1,0:T(8,128)(2,1)} %bitcast.9.wk_ref, bf16[2048,1024]{1,0:T(8,128)(2,1)S(1)} %bitcast.51, bf16[2048,8]{1,0:T(8,128)(2,1)S(1)} %copy-done.4, ...), custom_call_target="tpu_custom_call" | custom-call | tf_op jit(solution)/shard_map/verify_window/pallas_call | solution.py:239
  74.2 1.1 all_to_all.25
  75.4 5.3 %all-to-all-start.1 = ((bf16[4,12,7552]{2,1,0:T(8,128)(2,1)}), bf16[4,12,7552]{2,1,0:T(8,128)(2,1)}, u32[]{:S(2)}, u32[]{:S(2)}) async-start(bf16[4,12,7552]{2,1,0:T(8,128)(2,1)} %all_to_all.25), calls=%async_computation.2 | async-start | bytes 1933312 | tf_op jit(solution)/shard_map/all_to_all | solution.py:461
  80.7 1.5 collective-permute-start.3
  82.1 0.9 collective-permute-start.4
  83.1 2.0 collective-permute-start.5
  85.1 1.6 fusion.18
  86.7 16.1 %all-to-all-done.1 = bf16[4,12,7552]{2,1,0:T(8,128)(2,1)} async-done(((bf16[4,12,7552]{2,1,0:T(8,128)(2,1)}), bf16[4,12,7552]{2,1,0:T(8,128)(2,1)}, u32[]{:S(2)}, u32[]{:S(2)}) %all-to-all-start.1) | async-done | bytes 725024 | tf_op jit(solution)/shard_map/all_to_all | solution.py:461
  102.8 2.2 %all_to_all.27.refs_8_ = bf16[48,7552]{1,0:T(8,128)(2,1)} reshape(bf16[4,12,7552]{2,1,0:T(8,128)(2,1)} %all-to-all-done.1) | data formatting | bytes 1449984 | tf_op jit(solution)/shard_map/all_to_all | solution.py:461
  110.0 0.9 conditional.5
  110.0 0.9 broadcast.245
  110.9 0.9 conditional.4
  111.8 0.9 conditional.3
  111.8 0.9 broadcast.243
  112.8 57.4 %collective-permute-done.3.refs_13_.refs_14_.refs_15_.refs_16_ = bf16[8,4,128,128]{3,2,1,0:T(8,128)(2,1)S(1)} collective-permute-done((bf16[8,4,128,128]{3,2,1,0:T(8,128)(2,1)}, bf16[8,4,128,128]{3,2,1,0:T(8,128)(2,1)S(1)}, u32[]{:S(2)}, u32[]{:S(2)}) %collective-permute-start.3) | collective-permute-done | bytes 1048608 | tf_op jit(solution)/shard_map/ppermute | solution.py:427
  170.2 21.6 %collective-permute-done.4.refs_17_.refs_18_.refs_19_.refs_20_ = bf16[8,4,128,128]{3,2,1,0:T(8,128)(2,1)} collective-permute-done((bf16[8,4,128,128]{3,2,1,0:T(8,128)(2,1)}, bf16[8,4,128,128]{3,2,1,0:T(8,128)(2,1)}, u32[]{:S(2)}, u32[]{:S(2)}) %collective-permute-start.4) | collective-permute-done | bytes 1048608 | tf_op jit(solution)/shard_map/ppermute | solution.py:427
  191.8 1.9 collective-permute-done.5.refs_21_.refs_22_.refs_23_.refs_24_
  193.7 1.1 copy-done.2
  194.9 16.1 %place_states.1 = (f32[32,4,128,128]{3,2,1,0:T(8,128)}, bf16[32,1536]{1,0:T(8,128)(2,1)S(1)}, bf16[32,1536]{1,0:T(8,128)(2,1)S(1)}) custom-call(s32[32]{0:T(128)S(1)} %get-tuple-element.94.kind_ref, s32[32]{0:T(128)S(1)} %squeeze.48.refs_0_, s32[32]{0:T(128)S(1)} %squeeze.49.refs_1_, s32[32]{0:T(128)S(1)} %squeeze.50.refs_2_, s32[32]{0:T(128)S(1)} %squeeze.51.refs_3_, ...), custom_call_target="tpu_custom_call" | custom-call | tf_op jit(solution)/shard_map/place_states/pallas_call | solution.py:330
  211.6 1.6 convert_element_type.52
  (78 shorter events, 9.1 us)
Async XLA Ops:
  7.2 78.0 %copy-start = (bf16[512,2048]{1,0:T(8,128)(2,1)S(1)}, bf16[512,2048]{1,0:T(8,128)(2,1)}, u32[]{:S(2)}) copy-start(bf16[512,2048]{1,0:T(8,128)(2,1)} %param.34) | copy-start | bytes 6291460
  22.7 4.5 %copy-start.11 = (f32[4]{0:T(128)S(1)}, f32[4]{0:T(128)}, u32[]{:S(2)}) copy-start(f32[4]{0:T(128)} %param.31) | copy-start | bytes 52
  22.7 4.7 %copy-start.12 = (f32[4]{0:T(128)S(1)}, f32[4]{0:T(128)}, u32[]{:S(2)}) copy-start(f32[4]{0:T(128)} %param.32) | copy-start | bytes 52
  22.7 4.9 %copy-start.13 = (s32[32]{0:T(128)S(1)}, s32[32]{0:T(128)}, u32[]{:S(2)}) copy-start(s32[32]{0:T(128)} %param.35) | copy-start | bytes 388
  22.7 5.0 %copy-start.9 = (bf16[2048,4,2]{0,2,1:T(2,128)(2,1)S(1)}, bf16[2048,4,2]{0,2,1:T(2,128)(2,1)}, u32[]{:S(2)}) copy-start(bf16[2048,4,2]{0,2,1:T(2,128)(2,1)} %param.25) | copy-start | bytes 98308
  22.7 36.7 %all-to-all-start = ((bf16[256,8,512]{2,0,1:T(8,128)(2,1)}), bf16[256,8,512]{2,0,1:T(8,128)(2,1)}, u32[]{:S(2)}, u32[]{:S(2)}) async-start(bf16[256,8,512]{2,0,1:T(8,128)(2,1)} %bitcast.56), calls=%async_computation | async-start | bytes 4194304 | tf_op jit(solution)/shard_map/all_to_all | solution.py:432
  28.7 5.4 %copy-start.10 = (s32[32]{0:T(128)S(1)}, s32[32]{0:T(128)}, u32[]{:S(2)}) copy-start(s32[32]{0:T(128)} %param.36) | copy-start | bytes 388
  28.7 5.4 %copy-start.14 = (s32[32]{0:T(128)S(1)}, s32[32]{0:T(128)}, u32[]{:S(2)}) copy-start(s32[32]{0:T(128)} %param.37) | copy-start | bytes 388
  28.7 7.0 %copy-start.8 = (bf16[32,5,256]{2,0,1:T(8,128)(2,1)S(1)}, bf16[32,5,256]{2,0,1:T(8,128)(2,1)}, u32[]{:S(2)}) copy-start(bf16[32,5,256]{2,0,1:T(8,128)(2,1)} %param.22) | copy-start | bytes 245764
  28.7 30.7 %copy-start.5 = (bf16[32,3,512]{2,0,1:T(8,128)(2,1)S(1)}, bf16[32,3,512]{2,0,1:T(8,128)(2,1)}, u32[]{:S(2)}) copy-start(bf16[32,3,512]{2,0,1:T(8,128)(2,1)} %param.29) | copy-start | bytes 294916
  28.7 30.7 %copy-start.6 = (bf16[4,512]{1,0:T(4,128)(2,1)S(1)}, bf16[4,512]{1,0:T(4,128)(2,1)}, u32[]{:S(2)}) copy-start(bf16[4,512]{1,0:T(4,128)(2,1)} %cv_ref.1) | copy-start | bytes 12292
  28.7 30.7 %copy-start.7 = (f32[128]{0:T(128)S(1)}, f32[128]{0:T(128)}, u32[]{:S(2)}) copy-start(f32[128]{0:T(128)} %param.33) | copy-start | bytes 1540
  59.4 2.2 copy-start.1
  61.6 1.1 copy-start.3
  62.7 1.0 copy-start.4
  75.4 27.5 %all-to-all-start.1 = ((bf16[4,12,7552]{2,1,0:T(8,128)(2,1)}), bf16[4,12,7552]{2,1,0:T(8,128)(2,1)}, u32[]{:S(2)}, u32[]{:S(2)}) async-start(bf16[4,12,7552]{2,1,0:T(8,128)(2,1)} %all_to_all.25), calls=%async_computation.2 | async-start | bytes 1933312 | tf_op jit(solution)/shard_map/all_to_all | solution.py:461
  80.7 131.0 %reduce-scatter.2.cloned.1.call-start = ((), (), s32[]{:S(2)}) async-start(), calls=%async_computation.3 | async-start | bytes 1474560 | tf_op jit(solution)/shard_map/reduce_scatter | solution.py:459
  80.7 89.6 %collective-permute-start.3 = (bf16[8,4,128,128]{3,2,1,0:T(8,128)(2,1)}, bf16[8,4,128,128]{3,2,1,0:T(8,128)(2,1)S(1)}, u32[]{:S(2)}, u32[]{:S(2)}) collective-permute-start(bf16[8,4,128,128]{3,2,1,0:T(8,128)(2,1)} %pack_states.9), channel_id=1, source_target_pairs={{0,1},{1,2},{2,3},{3,0},{4,5},{5,6},{6,7},{7,4},{8,9},{9,10},{10,1... | collective-permute-start | bytes 3145736 | tf_op jit(solution)/shard_map/ppermute | solution.py:427
  82.1 109.7 %collective-permute-start.4 = (bf16[8,4,128,128]{3,2,1,0:T(8,128)(2,1)}, bf16[8,4,128,128]{3,2,1,0:T(8,128)(2,1)}, u32[]{:S(2)}, u32[]{:S(2)}) collective-permute-start(bf16[8,4,128,128]{3,2,1,0:T(8,128)(2,1)} %pack_states.10), channel_id=1, source_target_pairs={{0,2},{1,3},{2,0},{3,1},{4,6},{5,7},{6,4},{7,5},{8,10},{9,11},{10,... | collective-permute-start | bytes 3145736 | tf_op jit(solution)/shard_map/ppermute | solution.py:427
  83.1 110.7 %collective-permute-start.5 = (bf16[8,4,128,128]{3,2,1,0:T(8,128)(2,1)}, bf16[8,4,128,128]{3,2,1,0:T(8,128)(2,1)}, u32[]{:S(2)}, u32[]{:S(2)}) collective-permute-start(bf16[8,4,128,128]{3,2,1,0:T(8,128)(2,1)} %pack_states.11), channel_id=1, source_target_pairs={{0,3},{1,0},{2,1},{3,2},{4,7},{5,4},{6,5},{7,6},{8,11},{9,8},{10,9... | collective-permute-start | bytes 3145736 | tf_op jit(solution)/shard_map/ppermute | solution.py:427
  193.7 1.1 copy-start.2
Sparse Core Ops, SparseCore 0:
  86.9 35.4 reduce-scatter.1

commit v3 on v2

--- a/solution.py
+++ b/solution.py
@@ -77,7 +77,6 @@
     nw_ref,
     acc_ref,
     oh_ref,
-    plan_ref,
     st_ref,
     normed_ref,
     pay_ref,
@@ -217,19 +216,14 @@
                     p_s[:, at : at + size] = (kept_coef[j] * deltas[j]).astype(BF16)
                 at = o_scale + h * size
                 p_s[:, at : at + size] = jnp.broadcast_to(kept_whole, (requests, size)).astype(BF16)
-        width = p_s.shape[1]
-        pay_ref[:, :width] = jnp.dot(oh_ref[...], p_s[...], preferred_element_type=F32).astype(BF16)
-        pay_ref[:, width:] = jnp.broadcast_to(
-            plan_ref[...], (pay_ref.shape[0], plan_ref.shape[1])
-        ).astype(BF16)
-
-
-def verify(dims, x, wk, wv, wg, ck, cv, ks, vs, al, db, nw, acc, oh, plan, states):
+        pay_ref[...] = jnp.dot(oh_ref[...], p_s[...], preferred_element_type=F32).astype(BF16)
+
+
+def verify(dims, x, wk, wv, wg, ck, cv, ks, vs, al, db, nw, acc, oh, states):
     requests, window, heads, key_heads, size, span, needed, batch, slots = dims
     rows = requests * window
     width = layout(key_heads, heads, window, span, size, needed)[-1]
-    small = [x, wk, wv, wg, ck, cv, ks, vs, al, db, nw, acc, oh, plan]
-    sent = width + plan.shape[1]
+    small = [x, wk, wv, wg, ck, cv, ks, vs, al, db, nw, acc, oh]
 
     def whole(shape):
         return pl.BlockSpec(
@@ -240,14 +234,14 @@
         functools.partial(verify_kernel, dims),
         out_shape=(
             jax.ShapeDtypeStruct((rows, heads * size), BF16),
-            jax.ShapeDtypeStruct((oh.shape[0], sent), BF16),
+            jax.ShapeDtypeStruct((oh.shape[0], width), BF16),
         ),
         grid=(requests // batch,),
         in_specs=[whole(a.shape) for a in small]
         + [pl.BlockSpec((batch,) + states.shape[1:], lambda i: (i, 0, 0, 0))],
         out_specs=(
             pl.BlockSpec((rows, heads * size), lambda i: (0, 0)),
-            pl.BlockSpec((oh.shape[0], sent), lambda i: (0, 0)),
+            pl.BlockSpec((oh.shape[0], width), lambda i: (0, 0)),
         ),
         scratch_shapes=[
             pltpu.VMEM((key_heads, requests * slots, size), F32),
@@ -299,14 +293,19 @@
     def apply(slot, source_ref):
         index = step * batch + slot
         row = pl.multiple_of(index * lines, lines)
-        for h in range(heads):
-            k = k_s[h // ratio, pl.ds(row, lines), :].astype(BF16)
-            d = d_s[h, pl.ds(row, lines), :].astype(BF16)
+        for kh in range(key_heads):
+            k = k_s[kh, pl.ds(row, lines), :].astype(BF16)
+            d = jnp.concatenate(
+                [d_s[kh * ratio + e, pl.ds(row, lines), :] for e in range(ratio)], axis=1
+            ).astype(BF16)
             update = lax.dot_general(
                 k, d, (((0,), (0,)), ((), ())), preferred_element_type=F32
             )
-            weight = w_s[h, pl.ds(index, 1), :]
-            out_ref[slot, h] = weight * source_ref[0, h].astype(F32) + update
+            for e in range(ratio):
+                h = kh * ratio + e
+                weight = w_s[h, pl.ds(index, 1), :]
+                part = update[:, e * size : (e + 1) * size]
+                out_ref[slot, h] = weight * source_ref[0, h].astype(F32) + part
 
     for slot in range(batch):
         kind = kind_ref[step * batch + slot]
@@ -417,22 +416,33 @@
             picked[:, :share], (group + shift) % groups, 0, keepdims=False
         )
         sends[shift] = pack(states, rows_out)
-    sends, hidden, w_key, w_value, w_gates, key_conv_state, value_conv_state = (
+    last = order[-1]
+    own_plan = jnp.stack([next_group, next_slot])
+    sends[last], own_plan, hidden, w_key, w_value, w_gates, key_conv_state, value_conv_state = (
         lax.optimization_barrier(
-            (sends, hidden, w_key, w_value, w_gates, key_conv_state, value_conv_state)
+            (
+                sends[last],
+                own_plan,
+                hidden,
+                w_key,
+                w_value,
+                w_gates,
+                key_conv_state,
+                value_conv_state,
+            )
         )
     )
     base = {}
+    plans = [own_plan]
     for shift in order:
         base[shift] = lax.ppermute(sends[shift], "req", moves[shift])
+    for shift in range(1, groups):
+        plans.append(lax.ppermute(own_plan, "req", moves[shift]))
 
     own_rows = jnp.swapaxes(hidden, 0, 1).reshape(rows, feature_piece)
     gathered = lax.all_gather(own_rows, "head", axis=0)
     spread = spread_heads(w_key, devices, key_heads, pair_width)
     columns = lax.all_to_all(spread, "head", split_axis=1, concat_axis=0, tiled=True)
-    own_plan = jnp.concatenate([next_group, next_slot]).astype(F32)
-    own_plan = jnp.pad(own_plan, (0, -own_plan.shape[0] % 128))[None, :]
-
     local_state = lax.dynamic_slice_in_dim(key_conv_state, column_start, needed, 2)
     local_taps = lax.dynamic_slice_in_dim(conv_key, column_start, needed, 1)
     send_rows = matched.reshape(groups * CAP, requests).astype(BF16)
@@ -452,17 +462,17 @@
         norm_weight[None, :],
         accepted[:, None],
         send_rows,
-        own_plan,
         states,
     )
     partial_out = jnp.dot(normed, w_out, preferred_element_type=F32)
     mixed = lax.psum_scatter(partial_out, "head", scatter_dimension=1, tiled=True).astype(BF16)
     mixed = jnp.swapaxes(mixed.reshape(window, requests, -1), 0, 1)
     pay_in = lax.all_to_all(pay, "req", split_axis=0, concat_axis=0, tiled=True)
-    plan_at = pay.shape[1] - own_plan.shape[1]
-    plan = pay_in[::CAP, plan_at : plan_at + 2 * requests].astype(jnp.int32)
-    plan = plan.reshape(groups, 2, requests)
-
+
+    plan = jnp.stack(plans)
+    came = (group - jnp.arange(groups, dtype=jnp.int32) + groups) % groups
+    arrived = came[:, None] == jnp.arange(groups, dtype=jnp.int32)[None, :]
+    plan = jnp.sum(jnp.where(arrived[:, :, None, None], plan[None], 0), axis=1)
     groups_of, slots_of = plan[:, 0], plan[:, 1]
     mine = (groups_of == group).astype(jnp.int32)
     ranks = jnp.cumsum(mine, axis=1) - mine
@@ -520,6 +530,7 @@
     coded = lax.cummax(coded.reshape(2 * groups - 1, requests // batch, batch), axis=1)
     indexes = lax.rem(coded, limit).reshape(2 * groups - 1, requests)
     dims = (requests, window, heads, key_heads, size, span, needed, 8, batch)
+    kind, mixed = lax.optimization_barrier((kind, mixed))
     new_states, key_rows, value_rows = place(
         dims,
         kind,

time: 221 us -> 172 us (0.78)
  the two profiles are of different devices: /device:TPU:8 before, /device:TPU:0 now
where the time goes in v3:
time: 172 us; the launch traced here: 171 us
  waiting for transfers between devices  47.1 us (27%)
  Pallas kernels  36.2 us (21%)
  local copies, waits for them, and re-layouts  27 us (16%)
  starting transfers between devices  20.7 us (12%)
  between operations  16.3 us (9%)
  blocking collectives  15.4 us (9%)
  other arithmetic  6.49 us (4%)
    all_to_all x1, waiting for transfers between devices, local(): pay_in = lax.all_to_all(pay, 'req', split_axis=0, concat_axis=0, tiled=True)  47.1 us
    pallas_call x1, Pallas kernels, place(): pl.pallas_call(functools.partial(place_kernel, dims, count), out_shape=(j...  16 us
    all_gather x1, blocking collectives, local(): gathered = lax.all_gather(own_rows, 'head', axis=0)  15.4 us
    unnamed x30, local copies, waits for them, and re-layouts  12.3 us
    pallas_call x1, Pallas kernels, verify(): pl.pallas_call(functools.partial(verify_kernel, dims), out_shape=(jax.Sha...  10.6 us
    pallas_call x3, Pallas kernels, pack(): pl.pallas_call(pack_kernel, out_shape=jax.ShapeDtypeStruct((count,) + blo...  9.64 us
    ppermute x3, starting transfers between devices, local(): base[shift] = lax.ppermute(sends[shift], 'req', moves[shift])  5.92 us
    ppermute x3, starting transfers between devices, local(): plans.append(lax.ppermute(own_plan, 'req', moves[shift]))  5.29 us
  transfers between devices with their start and end apart: 9, of which 1 were waited for; matrix products, arithmetic and copies ran while one was open for 10% of the time, Pallas kernels for 10%

profile of v3, /device:TPU:0, one launch (start us, length us, event | category | flops | bytes accessed | tf_op | source)
XLA Modules:
  0.0 170.7 jit_solution(9818699696601082333)
XLA Ops:
  11.0 3.0 %pack_states.9 = bf16[8,4,128,128]{3,2,1,0:T(8,128)(2,1)} custom-call(s32[8]{0:T(128)} %get-tuple-element.113.index_ref, f32[32,4,128,128]{3,2,1,0:T(8,128)} %refs_12_.1, f32[32,4,128,128]{3,2,1,0:T(8,128)} %refs_12_.1, f32[32,4,128,128]{3,2,1,0:T(8,128)} %refs_12_.1, f32[32,4,128,128]{3,2,1,0:T(8,128)} %refs_12_.1), custom_call_target="tpu_custom_call" | custom-call | tf_op jit(solution)/shard_map/pack_states/pallas_call | solution.py:40
  14.1 3.1 %copy.48 = bf16[32,8,8,512]{3,2,0,1:T(8,128)(2,1)} copy(bf16[32,8,8,512]{3,2,1,0:T(8,128)(2,1)} %bitcast.58) | data formatting | bytes 4194304 | tf_op jit(solution)/shard_map/all_to_all | solution.py:445
  17.2 5.2 %all-to-all-start = ((bf16[256,8,512]{2,0,1:T(8,128)(2,1)}), bf16[256,8,512]{2,0,1:T(8,128)(2,1)}, u32[]{:S(2)}, u32[]{:S(2)}) async-start(bf16[256,8,512]{2,0,1:T(8,128)(2,1)} %bitcast.56), calls=%async_computation | async-start | bytes 4194304 | tf_op jit(solution)/shard_map/all_to_all | solution.py:445
  22.4 4.3 %collective-permute-start.5 = (s32[2,32]{1,0:T(2,128)S(1)}, s32[2,32]{1,0:T(2,128)S(1)}, u32[]{:S(2)}, u32[]{:S(2)}) collective-permute-start(s32[2,32]{1,0:T(2,128)S(1)} %pad_add_fusion.1), channel_id=1, source_target_pairs={{0,3},{1,0},{2,1},{3,2},{4,7},{5,4},{6,5},{7,6},{8,11},{9,8},{10,9... | collective-permute-start | bytes 776 | tf_op jit(solution)/shard_map/ppermute | solution.py:440
  26.7 1.0 collective-permute-start.3
  27.7 2.8 %collective-permute-start.8 = (bf16[8,4,128,128]{3,2,1,0:T(8,128)(2,1)}, bf16[8,4,128,128]{3,2,1,0:T(8,128)(2,1)S(1)}, u32[]{:S(2)}, u32[]{:S(2)}) collective-permute-start(bf16[8,4,128,128]{3,2,1,0:T(8,128)(2,1)} %pack_states.9), channel_id=1, source_target_pairs={{0,3},{1,0},{2,1},{3,2},{4,7},{5,4},{6,5},{7,6},{8,11},{9,8},{10,9... | collective-permute-start | bytes 3145736 | tf_op jit(solution)/shard_map/ppermute | solution.py:438
  30.5 3.4 %pack_states.10 = bf16[8,4,128,128]{3,2,1,0:T(8,128)(2,1)} custom-call(s32[8]{0:T(128)} %get-tuple-element.112.index_ref, f32[32,4,128,128]{3,2,1,0:T(8,128)} %refs_12_.1, f32[32,4,128,128]{3,2,1,0:T(8,128)} %refs_12_.1, f32[32,4,128,128]{3,2,1,0:T(8,128)} %refs_12_.1, f32[32,4,128,128]{3,2,1,0:T(8,128)} %refs_12_.1), custom_call_target="tpu_custom_call" | custom-call | tf_op jit(solution)/shard_map/pack_states/pallas_call | solution.py:40
  34.4 3.2 %pack_states.11 = bf16[8,4,128,128]{3,2,1,0:T(8,128)(2,1)} custom-call(s32[8]{0:T(128)} %get-tuple-element.111.index_ref, f32[32,4,128,128]{3,2,1,0:T(8,128)} %refs_12_.1, f32[32,4,128,128]{3,2,1,0:T(8,128)} %refs_12_.1, f32[32,4,128,128]{3,2,1,0:T(8,128)} %refs_12_.1, f32[32,4,128,128]{3,2,1,0:T(8,128)} %refs_12_.1), custom_call_target="tpu_custom_call" | custom-call | tf_op jit(solution)/shard_map/pack_states/pallas_call | solution.py:40
  38.4 0.9 dynamic-slice_bitcast_fusion.3.ks_ref
  39.3 15.4 %all_gather.3.x_ref = bf16[8,160,256]{2,1,0:T(8,128)(2,1)} all-gather(bf16[1,160,256]{2,1,0:T(8,128)(2,1)S(1)} %bitcast.60), channel_id=1, replica_groups=mesh['head'=8,'req'=4] {'head'}, dimensions={0}, use_global_device_ids=true | all-gather | bytes 737280 | tf_op jit(solution)/shard_map/all_gather | solution.py:443
  54.8 1.0 copy.37.wg_ref
  55.8 5.3 %copy.44 = bf16[256,8,4,256]{3,1,2,0:T(8,128)(2,1)} copy(bf16[256,8,4,256]{3,2,1,0:T(4,128)(2,1)} %bitcast.57) | data formatting | bytes 8388608
  61.1 3.1 %collective-permute-start.7 = (bf16[8,4,128,128]{3,2,1,0:T(8,128)(2,1)}, bf16[8,4,128,128]{3,2,1,0:T(8,128)(2,1)}, u32[]{:S(2)}, u32[]{:S(2)}) collective-permute-start(bf16[8,4,128,128]{3,2,1,0:T(8,128)(2,1)} %pack_states.11), channel_id=1, source_target_pairs={{0,2},{1,3},{2,0},{3,1},{4,6},{5,7},{6,4},{7,5},{8,10},{9,11},{10,... | collective-permute-start | bytes 3145736 | tf_op jit(solution)/shard_map/ppermute | solution.py:438
  64.4 2.2 %copy-done.1 = bf16[256,8,4,256]{3,1,2,0:T(8,128)(2,1)S(1)} copy-done((bf16[256,8,4,256]{3,1,2,0:T(8,128)(2,1)S(1)}, bf16[256,8,4,256]{3,1,2,0:T(8,128)(2,1)}, u32[]{:S(2)}) %copy-start.1) | copy-done | bytes 4194328
  66.5 1.1 copy-done.3
  67.6 1.0 copy-done.4
  68.7 10.6 %verify_window.1 = (bf16[160,512]{1,0:T(8,128)(2,1)S(1)}, bf16[48,7424]{1,0:T(8,128)(2,1)S(1)}) custom-call(bf16[8,160,256]{2,1,0:T(8,128)(2,1)S(1)} %copy-done.3, bf16[2048,512]{1,0:T(8,128)(2,1)} %bitcast.15.wk_ref, bf16[2048,1024]{1,0:T(8,128)(2,1)S(1)} %bitcast.51, bf16[2048,8]{1,0:T(8,128)(2,1)S(1)} %copy-done.4, ...), custom_call_target="tpu_custom_call" | custom-call | tf_op jit(solution)/shard_map/verify_window/pallas_call | solution.py:233
  79.2 0.8 copy-done.5
  80.1 1.6 fusion.19
  82.4 2.3 %all_to_all.25 = bf16[4,12,7424]{2,1,0:T(8,128)(2,1)} reshape(bf16[48,7424]{1,0:T(8,128)(2,1)} %copy-done.5) | data formatting | bytes 1425408 | tf_op jit(solution)/shard_map/all_to_all | solution.py:470
  84.6 4.2 %all-to-all-start.1 = ((bf16[4,12,7424]{2,1,0:T(8,128)(2,1)}), bf16[4,12,7424]{2,1,0:T(8,128)(2,1)}, u32[]{:S(2)}, u32[]{:S(2)}) async-start(bf16[4,12,7424]{2,1,0:T(8,128)(2,1)} %all_to_all.25), calls=%async_computation.2 | async-start | bytes 1900544 | tf_op jit(solution)/shard_map/all_to_all | solution.py:470
  92.5 0.9 conditional.5
  92.5 0.9 broadcast.293
  93.4 0.9 conditional.4
  93.4 0.9 broadcast.292
  94.3 0.9 conditional.3
  94.3 0.9 broadcast.291
  95.2 47.1 %all-to-all-done.1 = bf16[4,12,7424]{2,1,0:T(8,128)(2,1)} async-done(((bf16[4,12,7424]{2,1,0:T(8,128)(2,1)}), bf16[4,12,7424]{2,1,0:T(8,128)(2,1)}, u32[]{:S(2)}, u32[]{:S(2)}) %all-to-all-start.1) | async-done | bytes 712736 | tf_op jit(solution)/shard_map/all_to_all | solution.py:470
  142.2 2.2 %all_to_all.27.refs_8_ = bf16[48,7424]{1,0:T(8,128)(2,1)} reshape(bf16[4,12,7424]{2,1,0:T(8,128)(2,1)} %all-to-all-done.1) | data formatting | bytes 1425408 | tf_op jit(solution)/shard_map/all_to_all | solution.py:470
  144.5 1.6 convert_element_type.46
  146.1 1.1 copy-done.2
  147.2 16.0 %place_states.1 = (f32[32,4,128,128]{3,2,1,0:T(8,128)}, bf16[32,1536]{1,0:T(8,128)(2,1)S(1)}, bf16[32,1536]{1,0:T(8,128)(2,1)S(1)}) custom-call(s32[32]{0:T(128)S(1)} %get-tuple-element.66.kind_ref, s32[32]{0:T(128)S(1)} %squeeze.46.refs_0_, s32[32]{0:T(128)S(1)} %squeeze.47.refs_1_, s32[32]{0:T(128)S(1)} %squeeze.48.refs_2_, s32[32]{0:T(128)S(1)} %squeeze.49.refs_3_, ...), custom_call_target="tpu_custom_call" | custom-call | tf_op jit(solution)/shard_map/place_states/pallas_call | solution.py:329
  (83 shorter events, 8.3 us)
Async XLA Ops:
  7.2 72.9 %copy-start = (bf16[512,2048]{1,0:T(8,128)(2,1)S(1)}, bf16[512,2048]{1,0:T(8,128)(2,1)}, u32[]{:S(2)}) copy-start(bf16[512,2048]{1,0:T(8,128)(2,1)} %param.34) | copy-start | bytes 6291460
  17.2 47.1 %all-to-all-start = ((bf16[256,8,512]{2,0,1:T(8,128)(2,1)}), bf16[256,8,512]{2,0,1:T(8,128)(2,1)}, u32[]{:S(2)}, u32[]{:S(2)}) async-start(bf16[256,8,512]{2,0,1:T(8,128)(2,1)} %bitcast.56), calls=%async_computation | async-start | bytes 4194304 | tf_op jit(solution)/shard_map/all_to_all | solution.py:445
  22.4 122.1 %reduce-scatter.2.cloned.1.call-start = ((), (), s32[]{:S(2)}) async-start(), calls=%async_computation.3 | async-start | bytes 1474560 | tf_op jit(solution)/shard_map/reduce_scatter | solution.py:468
  22.4 38.6 %collective-permute-start.5 = (s32[2,32]{1,0:T(2,128)S(1)}, s32[2,32]{1,0:T(2,128)S(1)}, u32[]{:S(2)}, u32[]{:S(2)}) collective-permute-start(s32[2,32]{1,0:T(2,128)S(1)} %pad_add_fusion.1), channel_id=1, source_target_pairs={{0,3},{1,0},{2,1},{3,2},{4,7},{5,4},{6,5},{7,6},{8,11},{9,8},{10,9... | collective-permute-start | bytes 776 | tf_op jit(solution)/shard_map/ppermute | solution.py:440
  26.7 37.5 %collective-permute-start.4 = (s32[2,32]{1,0:T(2,128)S(1)}, s32[2,32]{1,0:T(2,128)S(1)}, u32[]{:S(2)}, u32[]{:S(2)}) collective-permute-start(s32[2,32]{1,0:T(2,128)S(1)} %pad_add_fusion.1), channel_id=1, source_target_pairs={{0,2},{1,3},{2,0},{3,1},{4,6},{5,7},{6,4},{7,5},{8,10},{9,11},{10,... | collective-permute-start | bytes 776 | tf_op jit(solution)/shard_map/ppermute | solution.py:440
  26.7 37.5 %collective-permute-start.3 = (s32[2,32]{1,0:T(2,128)S(1)}, s32[2,32]{1,0:T(2,128)S(1)}, u32[]{:S(2)}, u32[]{:S(2)}) collective-permute-start(s32[2,32]{1,0:T(2,128)S(1)} %pad_add_fusion.1), channel_id=1, source_target_pairs={{0,1},{1,2},{2,3},{3,0},{4,5},{5,6},{6,7},{7,4},{8,9},{9,10},{10,1... | collective-permute-start | bytes 776 | tf_op jit(solution)/shard_map/ppermute | solution.py:440
  27.7 118.3 %collective-permute-start.8 = (bf16[8,4,128,128]{3,2,1,0:T(8,128)(2,1)}, bf16[8,4,128,128]{3,2,1,0:T(8,128)(2,1)S(1)}, u32[]{:S(2)}, u32[]{:S(2)}) collective-permute-start(bf16[8,4,128,128]{3,2,1,0:T(8,128)(2,1)} %pack_states.9), channel_id=1, source_target_pairs={{0,3},{1,0},{2,1},{3,2},{4,7},{5,4},{6,5},{7,6},{8,11},{9,8},{10,9... | collective-permute-start | bytes 3145736 | tf_op jit(solution)/shard_map/ppermute | solution.py:438
  30.5 3.4 %copy-start.11 = (f32[4]{0:T(128)S(1)}, f32[4]{0:T(128)}, u32[]{:S(2)}) copy-start(f32[4]{0:T(128)} %param.31) | copy-start | bytes 52
  30.5 3.6 %copy-start.12 = (f32[4]{0:T(128)S(1)}, f32[4]{0:T(128)}, u32[]{:S(2)}) copy-start(f32[4]{0:T(128)} %param.32) | copy-start | bytes 52
  30.5 3.7 %copy-start.13 = (s32[32]{0:T(128)S(1)}, s32[32]{0:T(128)}, u32[]{:S(2)}) copy-start(s32[32]{0:T(128)} %param.35) | copy-start | bytes 388
  33.9 112.1 %collective-permute-start.6 = (bf16[8,4,128,128]{3,2,1,0:T(8,128)(2,1)}, bf16[8,4,128,128]{3,2,1,0:T(8,128)(2,1)}, u32[]{:S(2)}, u32[]{:S(2)}) collective-permute-start(bf16[8,4,128,128]{3,2,1,0:T(8,128)(2,1)} %pack_states.10), channel_id=1, source_target_pairs={{0,1},{1,2},{2,3},{3,0},{4,5},{5,6},{6,7},{7,4},{8,9},{9,10},{10,1... | collective-permute-start | bytes 3145736 | tf_op jit(solution)/shard_map/ppermute | solution.py:438
  34.4 4.9 %copy-start.9 = (bf16[32,5,256]{2,0,1:T(8,128)(2,1)S(1)}, bf16[32,5,256]{2,0,1:T(8,128)(2,1)}, u32[]{:S(2)}) copy-start(bf16[32,5,256]{2,0,1:T(8,128)(2,1)} %param.22) | copy-start | bytes 245764
  34.4 20.3 %copy-start.10 = (bf16[2048,4,2]{0,2,1:T(2,128)(2,1)S(1)}, bf16[2048,4,2]{0,2,1:T(2,128)(2,1)}, u32[]{:S(2)}) copy-start(bf16[2048,4,2]{0,2,1:T(2,128)(2,1)} %param.25) | copy-start | bytes 98308
  55.8 8.5 %copy-start.6 = (bf16[32,3,512]{2,0,1:T(8,128)(2,1)S(1)}, bf16[32,3,512]{2,0,1:T(8,128)(2,1)}, u32[]{:S(2)}) copy-start(bf16[32,3,512]{2,0,1:T(8,128)(2,1)} %param.29) | copy-start | bytes 294916
  55.8 8.5 %copy-start.7 = (bf16[4,512]{1,0:T(4,128)(2,1)S(1)}, bf16[4,512]{1,0:T(4,128)(2,1)}, u32[]{:S(2)}) copy-start(bf16[4,512]{1,0:T(4,128)(2,1)} %cv_ref.1) | copy-start | bytes 12292
  55.8 8.5 %copy-start.8 = (f32[128]{0:T(128)S(1)}, f32[128]{0:T(128)}, u32[]{:S(2)}) copy-start(f32[128]{0:T(128)} %param.33) | copy-start | bytes 1540
  61.1 85.0 %collective-permute-start.7 = (bf16[8,4,128,128]{3,2,1,0:T(8,128)(2,1)}, bf16[8,4,128,128]{3,2,1,0:T(8,128)(2,1)}, u32[]{:S(2)}, u32[]{:S(2)}) collective-permute-start(bf16[8,4,128,128]{3,2,1,0:T(8,128)(2,1)} %pack_states.11), channel_id=1, source_target_pairs={{0,2},{1,3},{2,0},{3,1},{4,6},{5,7},{6,4},{7,5},{8,10},{9,11},{10,... | collective-permute-start | bytes 3145736 | tf_op jit(solution)/shard_map/ppermute | solution.py:438
  64.3 2.2 %copy-start.1 = (bf16[256,8,4,256]{3,1,2,0:T(8,128)(2,1)S(1)}, bf16[256,8,4,256]{3,1,2,0:T(8,128)(2,1)}, u32[]{:S(2)}) copy-start(bf16[256,8,4,256]{3,1,2,0:T(8,128)(2,1)} %copy.44) | copy-start | bytes 12582916
  66.5 1.1 copy-start.3
  67.6 1.0 copy-start.4
  79.2 0.9 copy-start.5
  84.6 57.6 %all-to-all-start.1 = ((bf16[4,12,7424]{2,1,0:T(8,128)(2,1)}), bf16[4,12,7424]{2,1,0:T(8,128)(2,1)}, u32[]{:S(2)}, u32[]{:S(2)}) async-start(bf16[4,12,7424]{2,1,0:T(8,128)(2,1)} %all_to_all.25), calls=%async_computation.2 | async-start | bytes 1900544 | tf_op jit(solution)/shard_map/all_to_all | solution.py:470
  146.0 1.1 copy-start.2
Sparse Core Ops, SparseCore 0:
  81.8 35.4 reduce-scatter.1
